TPU v7x, 32 devices: a whole 2x2x4 slice. The times are simulated.
32 devices in a mesh: expert: 16 (over z, y, x), dp: 2 (over core).
Axes of the slice: x: 2, y: 2, z: 4, core: 2. Of those that a mesh axis runs over, the one named last changes fastest.
Arguments:
- tokens: bfloat16 [512, 7168], P('expert', 'dp'), may hold values from -6 to 6
- cotangent: bfloat16 [512, 7168], P('expert', 'dp'), may hold values from -6 to 6
- expert_ids: int32 [512, 8], P('expert'), may hold values from 0 to 15, all different within a row; in each aligned block of 32 rows (0 to 31, 32 to 63, ...) at most 32 rows name the same one
- route_weight: float32 [512, 8], P('expert'), may hold values from 0.1 to 1
- gate_weight: bfloat16 [16, 7168, 1024], P('expert', 'dp'), may hold values from -0.0625 to 0.0625
- up_weight: bfloat16 [16, 7168, 1024], P('expert', 'dp'), may hold values from -0.0625 to 0.0625
- down_weight: bfloat16 [16, 7168, 1024], P('expert', 'dp'), may hold values from -0.1875 to 0.1875
Outputs:
- mixed: bfloat16 [512, 7168], P('expert', 'dp')
- grad_tokens: bfloat16 [512, 7168], P('expert', 'dp')
Inputs may be any that keep to these rules, and one draw needn't show every extreme that they name: `expert_ids`: each row names 8 different experts. In the rows of one device (aligned blocks of 32 rows) no expert is named more than 32 times, and in every draw some block names some expert exactly 32 times.
All inputs are finite; a program needn't handle non-finite values.
Results may differ from a plain program's by a relative error of at most 0.028.
Values may be sent and summed in bfloat16 or wider, within the bound.
No kernel may reach another device: no remote copies, remote signals or barrier semaphores. Data moves between devices by JAX's collectives and lax.ppermute only.
A program may use at most 64 MiB of HBM per device.

v0:
```python
import jax
import jax.numpy as jnp
from jax import lax
from jax.sharding import PartitionSpec as P


def activate(gate_sum, up_sum):
    return (gate_sum * jax.nn.sigmoid(gate_sum) * up_sum).astype(jnp.bfloat16)


def backprop(hidden_grad, gate_sum, up_sum):
    sig_gate = jax.nn.sigmoid(gate_sum)
    up_grad = (hidden_grad * gate_sum * sig_gate).astype(jnp.bfloat16)
    gate_grad = (hidden_grad * up_sum * sig_gate * (1.0 + gate_sum * (1.0 - sig_gate))).astype(
        jnp.bfloat16
    )
    return (gate_grad, up_grad)


def local(tokens, cotangent, expert_ids, route_weight, gate_weight, up_weight, down_weight):
    experts = lax.axis_size("expert")
    tok_count, share_width = tokens.shape
    top_count = expert_ids.shape[1]
    capacity = max(2, min(tok_count, 2 * tok_count * top_count // experts))
    flat_ids = expert_ids.reshape(-1)
    onehot = (flat_ids[:, None] == jnp.arange(experts, dtype=jnp.int32)[None, :]).astype(jnp.int32)
    before = jnp.cumsum(onehot, axis=0) - onehot
    target = flat_ids * capacity + jnp.sum(before * onehot, axis=1)
    flat_weight = route_weight.reshape(-1)
    token_rows = jnp.repeat(tokens, top_count, axis=0)
    grad_rows = (
        flat_weight[:, None] * jnp.repeat(cotangent, top_count, axis=0).astype(jnp.float32)
    ).astype(jnp.bfloat16)
    empty = jnp.zeros((experts * capacity, share_width), jnp.bfloat16)
    send_tokens = empty.at[target].set(token_rows)
    send_grads = empty.at[target].set(grad_rows)
    routed_tokens, routed_grads = (
        lax.all_to_all(send_tokens, "expert", split_axis=0, concat_axis=0, tiled=True),
        lax.all_to_all(send_grads, "expert", split_axis=0, concat_axis=0, tiled=True),
    )
    gate_w = gate_weight[0]
    up_w = up_weight[0]
    down_w = down_weight[0]
    gate_part = jnp.dot(routed_tokens, gate_w, preferred_element_type=jnp.float32)
    up_part = jnp.dot(routed_tokens, up_w, preferred_element_type=jnp.float32)
    hidden_part = jnp.dot(routed_grads, down_w, preferred_element_type=jnp.float32)
    gate_sum, up_sum = (
        lax.psum(gate_part.astype(jnp.bfloat16), "dp").astype(jnp.float32),
        lax.psum(up_part.astype(jnp.bfloat16), "dp").astype(jnp.float32),
    )
    hidden = activate(gate_sum, up_sum)
    hidden_grad = lax.psum(hidden_part.astype(jnp.bfloat16), "dp").astype(jnp.float32)
    gate_grad, up_grad = backprop(hidden_grad, gate_sum, up_sum)
    contract = (((1,), (1,)), ((), ()))
    expert_out = lax.dot_general(
        hidden, down_w, contract, preferred_element_type=jnp.float32
    ).astype(jnp.bfloat16)
    slot_grad = (
        lax.dot_general(gate_grad, gate_w, contract, preferred_element_type=jnp.float32)
        + lax.dot_general(up_grad, up_w, contract, preferred_element_type=jnp.float32)
    ).astype(jnp.bfloat16)
    back_out, back_grad = (
        lax.all_to_all(expert_out, "expert", split_axis=0, concat_axis=0, tiled=True),
        lax.all_to_all(slot_grad, "expert", split_axis=0, concat_axis=0, tiled=True),
    )
    picked = back_out[target].astype(jnp.float32) * flat_weight[:, None]
    mixed = jnp.sum(picked.reshape(tok_count, top_count, share_width), axis=1).astype(jnp.bfloat16)
    grad_tokens = jnp.sum(
        back_grad[target].astype(jnp.float32).reshape(tok_count, top_count, share_width), axis=1
    ).astype(jnp.bfloat16)
    return (mixed, grad_tokens)


def solution(mesh):
    return jax.shard_map(
        local,
        mesh=mesh,
        in_specs=(
            P("expert", "dp"),
            P("expert", "dp"),
            P("expert", None),
            P("expert", None),
            P("expert", "dp", None),
            P("expert", "dp", None),
            P("expert", "dp", None),
        ),
        out_specs=(P("expert", "dp"), P("expert", "dp")),
        check_vma=False,
    )
```

profile of v0, /device:TPU:14, one launch (start us, length us, event | category | flops | bytes accessed | tf_op | source)
XLA Modules:
  0.0 434.0 jit_solution(1363337635020401089)
XLA Ops:
  7.2 0.0 copy-start
  7.2 0.8 copy.11
  8.0 0.1 eq.29
  8.1 0.1 eq.25
  8.2 0.7 broadcast_multiply_fusion
  8.9 0.6 reduce-window.6
  9.4 0.2 slice_reduce_fusion
  9.7 0.1 copy.10
  9.7 0.1 mul.64
  9.8 0.1 fusion.55
  9.9 0.0 copy-done
  9.9 5.5 %scatter_custom_fusion = bf16[512,3584]{1,0:T(8,128)(2,1)} fusion(s32[256]{0:T(256)S(1)} %bitcast.74, bf16[]{:T(256)} %constant.6.clone.1, bf16[32,3584]{1,0:T(8,128)(2,1)S(1)} %copy-done), kind=kCustom, calls=%fused_computation.40 | custom fusion | bytes 3899394 | tf_op jit(solution)/shard_map/scatter | solution.py:35
  15.4 0.0 copy-start.3
  15.4 0.0 copy-start.2
  15.4 7.3 %all-to-all-start = ((bf16[16,32,3584]{2,1,0:T(8,128)(2,1)}), bf16[16,32,3584]{2,1,0:T(8,128)(2,1)}, u32[]{:S(2)}, u32[]{:S(2)}) async-start(bf16[16,32,3584]{2,1,0:T(8,128)(2,1)} %bitcast.71), calls=%async_computation | async-start | bytes 7340032 | tf_op jit(solution)/shard_map/all_to_all | solution.py:38
  22.7 0.0 copy-done.3
  22.7 0.1 copy.14
  22.8 0.1 mul.70
  22.9 0.0 copy-done.2
  22.9 5.6 %scatter_custom_fusion.1 = bf16[512,3584]{1,0:T(8,128)(2,1)} fusion(s32[256]{0:T(256)S(1)} %bitcast.75, f32[32,3584]{1,0:T(8,128)S(1)} %convert_element_type.74, f32[256]{0:T(256)S(1)} %mul.70, bf16[]{:T(256)} %constant.6.clone.1), kind=kCustom, calls=%fused_computation.38 | custom fusion | flops 1835008 | bytes 4129794 | tf_op jit(solution)/shard_map/scatter | solution.py:36
  28.5 77.0 %all-to-all-done = bf16[16,32,3584]{2,1,0:T(8,128)(2,1)} async-done(((bf16[16,32,3584]{2,1,0:T(8,128)(2,1)}), bf16[16,32,3584]{2,1,0:T(8,128)(2,1)}, u32[]{:S(2)}, u32[]{:S(2)}) %all-to-all-start) | async-done | bytes 3670048 | tf_op jit(solution)/shard_map/all_to_all | solution.py:38
  105.5 5.1 %all-to-all-start.2 = ((bf16[16,32,3584]{2,1,0:T(8,128)(2,1)}), bf16[16,32,3584]{2,1,0:T(8,128)(2,1)}, u32[]{:S(2)}, u32[]{:S(2)}) async-start(bf16[16,32,3584]{2,1,0:T(8,128)(2,1)} %bitcast.70), calls=%async_computation.2 | async-start | bytes 7340032 | tf_op jit(solution)/shard_map/all_to_all | solution.py:39
  110.6 0.2 all-reduce.3.cloned.1.call-start
  110.9 9.1 %fusion.37 = bf16[512,1024]{1,0:T(8,128)(2,1)} fusion(bf16[512,3584]{1,0:T(8,128)(2,1)} %bitcast.5, bf16[1,3584,1024]{2,1,0:T(8,128)(2,1)} %param.11), kind=kOutput, calls=%fused_computation.46 | convolution fusion | flops 3758620672 | bytes 12058624 | tf_op jit(solution)/shard_map/dot_general | solution.py:44
  120.0 9.1 %fusion.40 = bf16[512,1024]{1,0:T(8,128)(2,1)} fusion(bf16[512,3584]{1,0:T(8,128)(2,1)} %bitcast.5, bf16[1,3584,1024]{2,1,0:T(8,128)(2,1)} %param.12), kind=kOutput, calls=%fused_computation.47 | convolution fusion | flops 3758620672 | bytes 12058624 | tf_op jit(solution)/shard_map/dot_general | solution.py:45
  129.1 62.8 %all-to-all-done.2 = bf16[16,32,3584]{2,1,0:T(8,128)(2,1)} async-done(((bf16[16,32,3584]{2,1,0:T(8,128)(2,1)}), bf16[16,32,3584]{2,1,0:T(8,128)(2,1)}, u32[]{:S(2)}, u32[]{:S(2)}) %all-to-all-start.2) | async-done | bytes 3670048 | tf_op jit(solution)/shard_map/all_to_all | solution.py:39
  192.0 9.1 %fusion.43 = bf16[512,1024]{1,0:T(8,128)(2,1)} fusion(bf16[512,3584]{1,0:T(8,128)(2,1)} %bitcast.14, bf16[1,3584,1024]{2,1,0:T(8,128)(2,1)} %param.13), kind=kOutput, calls=%fused_computation.48 | convolution fusion | flops 3758620672 | bytes 12058624 | tf_op jit(solution)/shard_map/dot_general | solution.py:46
  201.1 0.0 all-reduce.3.cloned.1.call-update
  201.1 23.0 %all-reduce.3.cloned.1.call-done = (bf16[512,1024]{1,0:T(8,128)(2,1)}, bf16[512,1024]{1,0:T(8,128)(2,1)}, bf16[512,1024]{1,0:T(8,128)(2,1)}) async-done(((bf16[512,1024]{1,0:T(8,128)(2,1)}, bf16[512,1024]{1,0:T(8,128)(2,1)}, bf16[512,1024]{1,0:T(8,128)(2,1)}), (bf16[512,1024]{1,0:T(8,128)(2,1)}, bf16[512,1024]{1,0:T(8,128)(2,1)}, bf16[512,1024]{1,0:T(8,128)(2,1)})) %all-reduce.3.cloned.1.call-update) | async-done | bytes 3145744 | tf_op jit(solution)/shard_map/psum | solution.py:49
  224.1 0.0 copy-start.4
  224.1 0.0 copy-start.5
  224.1 0.0 copy-start.6
  224.1 7.8 %fusion.4 = f32[512,3584]{1,0:T(8,128)S(1)} fusion(bf16[1,3584,1024]{2,1,0:T(8,128)(2,1)} %param.12, bf16[512,1024]{1,0:T(8,128)(2,1)} %get-tuple-element.3, bf16[512,1024]{1,0:T(8,128)(2,1)} %get-tuple-element.4), kind=kOutput, calls=%fused_computation.8 | convolution fusion | flops 3762290688 | bytes 16777216 | tf_op jit(solution)/shard_map/dot_general | solution.py:60
  231.9 0.0 copy-done.4
  231.9 0.0 copy-done.5
  231.9 0.0 copy-done.6
  231.9 9.3 %add_convert_fusion = bf16[512,3584]{1,0:T(8,128)(2,1)} fusion(f32[512,3584]{1,0:T(8,128)S(1)} %fusion.4, bf16[1,3584,1024]{2,1,0:T(8,128)(2,1)} %param.11, bf16[512,1024]{1,0:T(8,128)(2,1)S(1)} %copy-done.4, bf16[512,1024]{1,0:T(8,128)(2,1)S(1)} %copy-done.6, bf16[512,1024]{1,0:T(8,128)(2,1)S(1)} %copy-done.5), kind=kOutput, calls=%fused_computation.16 | convolution fusion | flops 3768582144 | bytes 21495808 | tf_op jit(solution)/shard_map/dot_general | solution.py:59
  241.2 7.0 %all-to-all-start.3 = ((bf16[16,32,3584]{2,1,0:T(8,128)(2,1)}), bf16[16,32,3584]{2,1,0:T(8,128)(2,1)}, u32[]{:S(2)}, u32[]{:S(2)}) async-start(bf16[16,32,3584]{2,1,0:T(8,128)(2,1)} %bitcast.73), calls=%async_computation.3 | async-start | bytes 7340032 | tf_op jit(solution)/shard_map/all_to_all | solution.py:64
  248.2 8.8 %fusion.14 = bf16[512,3584]{1,0:T(8,128)(2,1)} fusion(bf16[1,3584,1024]{2,1,0:T(8,128)(2,1)} %param.13, bf16[512,1024]{1,0:T(8,128)(2,1)S(1)} %copy-done.4, bf16[512,1024]{1,0:T(8,128)(2,1)S(1)} %copy-done.5), kind=kOutput, calls=%fused_computation.17 | convolution fusion | flops 3764125696 | bytes 13107200 | tf_op jit(solution)/shard_map/dot_general | solution.py:55
  256.9 75.4 %all-to-all-done.3 = bf16[16,32,3584]{2,1,0:T(8,128)(2,1)} async-done(((bf16[16,32,3584]{2,1,0:T(8,128)(2,1)}), bf16[16,32,3584]{2,1,0:T(8,128)(2,1)}, u32[]{:S(2)}, u32[]{:S(2)}) %all-to-all-start.3) | async-done | bytes 3670048 | tf_op jit(solution)/shard_map/all_to_all | solution.py:64
  332.4 5.1 %all-to-all-start.1 = ((bf16[16,32,3584]{2,1,0:T(8,128)(2,1)}), bf16[16,32,3584]{2,1,0:T(8,128)(2,1)}, u32[]{:S(2)}, u32[]{:S(2)}) async-start(bf16[16,32,3584]{2,1,0:T(8,128)(2,1)} %bitcast.72), calls=%async_computation.1 | async-start | bytes 7340032 | tf_op jit(solution)/shard_map/all_to_all | solution.py:63
  337.5 6.0 %gather_fusion.1 = bf16[256,3584]{1,0:T(8,128)(2,1)S(1)} fusion(bf16[512,3584]{1,0:T(8,128)(2,1)} %bitcast.16, s32[1024]{0:T(1024)S(1)} %pad_clamp_fusion), kind=kCustom, calls=%fused_computation.1 | custom fusion | bytes 3671040 | tf_op jit(solution)/shard_map/gather | solution.py:69
  343.5 1.9 bitcast_reduce_fusion
  345.4 73.5 %all-to-all-done.1 = bf16[16,32,3584]{2,1,0:T(8,128)(2,1)} async-done(((bf16[16,32,3584]{2,1,0:T(8,128)(2,1)}), bf16[16,32,3584]{2,1,0:T(8,128)(2,1)}, u32[]{:S(2)}, u32[]{:S(2)}) %all-to-all-start.1) | async-done | bytes 3670048 | tf_op jit(solution)/shard_map/all_to_all | solution.py:63
  418.9 0.0 copy-start.1
  418.9 6.1 %gather_fusion = bf16[256,3584]{1,0:T(8,128)(2,1)S(1)} fusion(bf16[512,3584]{1,0:T(8,128)(2,1)} %bitcast.10, s32[1024]{0:T(1024)S(1)} %pad_clamp_fusion), kind=kCustom, calls=%fused_computation | custom fusion | bytes 3671040 | tf_op jit(solution)/shard_map/gather | solution.py:66
  425.0 2.1 fusion.17
  427.1 0.0 copy-done.1
  (6 shorter events, 0.1 us)
Async XLA Ops:
  7.2 2.8 copy-start
  15.4 7.3 %copy-start.3 = (f32[32,8]{0,1:T(8,128)S(1)}, f32[32,8]{0,1:T(8,128)}, u32[]{:S(2)}) copy-start(f32[32,8]{0,1:T(8,128)} %param.10) | copy-start | bytes 3076
  15.4 7.4 %copy-start.2 = (bf16[32,3584]{1,0:T(8,128)(2,1)S(1)}, bf16[32,3584]{1,0:T(8,128)(2,1)}, u32[]{:S(2)}) copy-start(bf16[32,3584]{1,0:T(8,128)(2,1)} %param.8) | copy-start | bytes 688132
  15.4 90.1 %all-to-all-start = ((bf16[16,32,3584]{2,1,0:T(8,128)(2,1)}), bf16[16,32,3584]{2,1,0:T(8,128)(2,1)}, u32[]{:S(2)}, u32[]{:S(2)}) async-start(bf16[16,32,3584]{2,1,0:T(8,128)(2,1)} %bitcast.71), calls=%async_computation | async-start | bytes 7340032 | tf_op jit(solution)/shard_map/all_to_all | solution.py:38
  105.5 86.4 %all-to-all-start.2 = ((bf16[16,32,3584]{2,1,0:T(8,128)(2,1)}), bf16[16,32,3584]{2,1,0:T(8,128)(2,1)}, u32[]{:S(2)}, u32[]{:S(2)}) async-start(bf16[16,32,3584]{2,1,0:T(8,128)(2,1)} %bitcast.70), calls=%async_computation.2 | async-start | bytes 7340032 | tf_op jit(solution)/shard_map/all_to_all | solution.py:39
  110.6 113.5 %all-reduce.3.cloned.1.call-start = ((), (), s32[]{:S(2)}) async-start(), calls=%async_computation.4 | async-start | bytes 6291456 | tf_op jit(solution)/shard_map/psum | solution.py:49
  224.1 7.8 %copy-start.4 = (bf16[512,1024]{1,0:T(8,128)(2,1)S(1)}, bf16[512,1024]{1,0:T(8,128)(2,1)}, u32[]{:S(2)}) copy-start(bf16[512,1024]{1,0:T(8,128)(2,1)} %get-tuple-element.2) | copy-start | bytes 3145732
  224.1 7.8 %copy-start.5 = (bf16[512,1024]{1,0:T(8,128)(2,1)S(1)}, bf16[512,1024]{1,0:T(8,128)(2,1)}, u32[]{:S(2)}) copy-start(bf16[512,1024]{1,0:T(8,128)(2,1)} %get-tuple-element.3) | copy-start | bytes 3145732
  224.1 7.8 %copy-start.6 = (bf16[512,1024]{1,0:T(8,128)(2,1)S(1)}, bf16[512,1024]{1,0:T(8,128)(2,1)}, u32[]{:S(2)}) copy-start(bf16[512,1024]{1,0:T(8,128)(2,1)} %get-tuple-element.4) | copy-start | bytes 3145732
  241.2 91.2 %all-to-all-start.3 = ((bf16[16,32,3584]{2,1,0:T(8,128)(2,1)}), bf16[16,32,3584]{2,1,0:T(8,128)(2,1)}, u32[]{:S(2)}, u32[]{:S(2)}) async-start(bf16[16,32,3584]{2,1,0:T(8,128)(2,1)} %bitcast.73), calls=%async_computation.3 | async-start | bytes 7340032 | tf_op jit(solution)/shard_map/all_to_all | solution.py:64
  332.4 86.5 %all-to-all-start.1 = ((bf16[16,32,3584]{2,1,0:T(8,128)(2,1)}), bf16[16,32,3584]{2,1,0:T(8,128)(2,1)}, u32[]{:S(2)}, u32[]{:S(2)}) async-start(bf16[16,32,3584]{2,1,0:T(8,128)(2,1)} %bitcast.72), calls=%async_computation.1 | async-start | bytes 7340032 | tf_op jit(solution)/shard_map/all_to_all | solution.py:63
  418.9 8.2 %copy-start.1 = (bf16[32,3584]{1,0:T(8,128)(2,1)S(1)}, bf16[32,3584]{1,0:T(8,128)(2,1)}, u32[]{:S(2)}) copy-start(bf16[32,3584]{1,0:T(8,128)(2,1)} %param.7) | copy-start | bytes 688132
Sparse Core Ops, SparseCore 0:
  201.2 22.8 all-reduce.2
where the time goes:
time: 435 us; the launch traced here: 434 us
  waiting for transfers between devices  312 us (72%)
  matrix products  53.3 us (12%)
  starting transfers between devices  24.7 us (6%)
  local copies, waits for them, and re-layouts  19.1 us (4%)
  between operations  14.1 us (3%)
  other arithmetic  11.1 us (3%)
    all_to_all x1, waiting for transfers between devices, local(): lax.all_to_all(send_tokens, 'expert', split_axis=0, concat_axis=0, tiled=...  77 us
    all_to_all x1, waiting for transfers between devices, local(): lax.all_to_all(slot_grad, 'expert', split_axis=0, concat_axis=0, tiled=True)  75.4 us
    all_to_all x1, waiting for transfers between devices, local(): lax.all_to_all(expert_out, 'expert', split_axis=0, concat_axis=0, tiled=T...  73.5 us
    all_to_all x1, waiting for transfers between devices, local(): lax.all_to_all(send_grads, 'expert', split_axis=0, concat_axis=0, tiled=T...  62.8 us
    psum x1, waiting for transfers between devices, local(): lax.psum(up_part.astype(jnp.bfloat16), 'dp').astype(jnp.float32)  23 us
    dot_general x1, matrix products, local(): lax.dot_general(gate_grad, gate_w, contract, preferred_element_type=jnp.f...  9.28 us
    dot_general x1, matrix products, local(): jnp.dot(routed_tokens, gate_w, preferred_element_type=jnp.float32)  9.15 us
    dot_general x1, matrix products, local(): jnp.dot(routed_grads, down_w, preferred_element_type=jnp.float32)  9.14 us
  transfers between devices with their start and end apart: 5, of which 5 were waited for; matrix products, arithmetic and copies ran while one was open for 9% of the time, Pallas kernels for 0%

commit v1 on v0

v1 whole, which is shorter than its diff:
```python
import jax
import jax.numpy as jnp
from jax import lax
from jax.sharding import PartitionSpec as P


def local(tokens, cotangent, expert_ids, route_weight, gate_weight, up_weight, down_weight):
    f32, bf16 = jnp.float32, jnp.bfloat16
    me = lax.axis_index("expert")
    gate_w = gate_weight[0]
    up_w = up_weight[0]
    down_w = down_weight[0]
    all_tokens = lax.all_gather(tokens, "expert", axis=0, tiled=True)
    all_cot = lax.all_gather(cotangent, "expert", axis=0, tiled=True)
    all_ids = lax.all_gather(expert_ids, "expert", axis=0, tiled=True)
    all_weight = lax.all_gather(route_weight, "expert", axis=0, tiled=True)
    chosen = all_ids == me
    weight = jnp.sum(jnp.where(chosen, all_weight, 0.0), axis=1, keepdims=True)
    named = jnp.any(chosen, axis=1, keepdims=True)
    gate_part = jnp.dot(all_tokens, gate_w, preferred_element_type=f32).astype(bf16)
    up_part = jnp.dot(all_tokens, up_w, preferred_element_type=f32).astype(bf16)
    hidden_part = (weight * jnp.dot(all_cot, down_w, preferred_element_type=f32)).astype(bf16)
    gate = lax.psum(gate_part, "dp").astype(f32)
    up = lax.psum(up_part, "dp").astype(f32)
    hidden_grad = lax.psum(hidden_part, "dp").astype(f32)
    sig = jax.nn.sigmoid(gate)
    hidden = (gate * sig * up).astype(bf16)
    up_grad = (hidden_grad * gate * sig).astype(bf16)
    gate_grad = (hidden_grad * up * sig * (1.0 + gate * (1.0 - sig))).astype(bf16)
    contract = (((1,), (1,)), ((), ()))
    out = (weight * lax.dot_general(hidden, down_w, contract, preferred_element_type=f32)).astype(bf16)
    grad = (
        lax.dot_general(gate_grad, gate_w, contract, preferred_element_type=f32)
        + lax.dot_general(up_grad, up_w, contract, preferred_element_type=f32)
    )
    grad = jnp.where(named, grad, 0.0).astype(bf16)
    mixed = lax.psum_scatter(out, "expert", scatter_dimension=0, tiled=True)
    grad_tokens = lax.psum_scatter(grad, "expert", scatter_dimension=0, tiled=True)
    return (mixed, grad_tokens)


def solution(mesh):
    return jax.shard_map(
        local,
        mesh=mesh,
        in_specs=(
            P("expert", "dp"),
            P("expert", "dp"),
            P("expert", None),
            P("expert", None),
            P("expert", "dp", None),
            P("expert", "dp", None),
            P("expert", "dp", None),
        ),
        out_specs=(P("expert", "dp"), P("expert", "dp")),
        check_vma=False,
    )
```

time: 435 us -> 393 us (0.903)
  blocking collectives: 0 us -> 69.3 us
  waiting for transfers between devices: 312 us -> 248 us
  starting transfers between devices: 24.7 us -> 0.38 us
  local copies, waits for them, and re-layouts: 19.1 us -> 0.18 us
  other arithmetic: 11.1 us -> 0.07 us
    all_to_all x4 -> x0, waiting for transfers between devices: 289 us -> none  [the longest x1 77 us: local(): lax.all_to_all(send_tokens, 'expert', split_axis=0, concat_axis=0, tiled=...]
    reduce_scatter x0 -> x2, waiting for transfers between devices: none -> 163 us  [the longest x1 87.1 us: local(): mixed = lax.psum_scatter(out, 'expert', scatter_dimension=0, tiled=True)]
    all_gather x0 -> x2, blocking collectives: none -> 69.3 us  [the longest x1 40.6 us: local(): all_weight = lax.all_gather(route_weight, 'expert', axis=0, tiled=True)]
    all_gather x0 -> x2, waiting for transfers between devices: none -> 61.3 us  [the longest x1 56.2 us: local(): all_cot = lax.all_gather(cotangent, 'expert', axis=0, tiled=True)]
    all_to_all x4 -> x0, starting transfers between devices: 24.5 us -> none  [the longest x1 7.27 us: local(): lax.all_to_all(send_tokens, 'expert', split_axis=0, concat_axis=0, tiled=...]
    gather x2 -> x0, local copies, waits for them, and re-layouts: 12.1 us -> none  [the longest x1 6.08 us: local(): picked = back_out[target].astype(jnp.float32) * flat_weight[:, None]]
    scatter x1 -> x0, other arithmetic: 5.61 us -> none  [local(): send_grads = empty.at[target].set(grad_rows)]
    scatter x1 -> x0, local copies, waits for them, and re-layouts: 5.48 us -> none  [local(): send_tokens = empty.at[target].set(token_rows)]
  transfers between devices with their start and end apart: 5 -> 5, of which waited for: 5 -> 5; matrix products, arithmetic and copies ran while one was open for 9% -> 7% of each run, Pallas kernels for 0% -> 0%
where the time goes in v1:
time: 393 us; the launch traced here: 388 us
  waiting for transfers between devices  248 us (63%)
  blocking collectives  69.3 us (18%)
  matrix products  56 us (14%)
  between operations  13.8 us (4%)
    reduce_scatter x1, waiting for transfers between devices, local(): mixed = lax.psum_scatter(out, 'expert', scatter_dimension=0, tiled=True)  87.1 us
    reduce_scatter x1, waiting for transfers between devices, local(): lax.psum_scatter(grad, 'expert', scatter_dimension=0, tiled=True)  75.5 us
    all_gather x1, waiting for transfers between devices, local(): all_cot = lax.all_gather(cotangent, 'expert', axis=0, tiled=True)  56.2 us
    all_gather x1, blocking collectives, local(): all_weight = lax.all_gather(route_weight, 'expert', axis=0, tiled=True)  40.6 us
    all_gather x1, blocking collectives, local(): all_ids = lax.all_gather(expert_ids, 'expert', axis=0, tiled=True)  28.6 us
    psum x1, waiting for transfers between devices, local(): up = lax.psum(up_part, 'dp').astype(f32)  23.1 us
    dot_general x1, matrix products, local(): lax.dot_general(up_grad, up_w, contract, preferred_element_type=f32)  10.9 us
    dot_general x1, matrix products, local(): lax.dot_general(gate_grad, gate_w, contract, preferred_element_type=f32)  10.3 us
  transfers between devices with their start and end apart: 5, of which 5 were waited for; matrix products, arithmetic and copies ran while one was open for 7% of the time, Pallas kernels for 0%

profile of v1, /device:TPU:14, one launch (start us, length us, event | category | flops | bytes accessed | tf_op | source)
XLA Modules:
  0.0 388.0 jit_solution(4316116910010661094)
XLA Ops:
  7.2 0.0 all-gather.5.cloned.1.call-start
  7.2 0.7 all-gather.5.cloned.1.call-update
  7.9 0.0 all-gather.7.cloned.1.call-start
  7.9 0.7 all-gather.7.cloned.1.call-update
  8.6 0.0 all-reduce.3.cloned.1.call-start
  8.7 28.6 %all-gather = s32[16,32,8]{1,2,0:T(8,128)S(1)} all-gather(s32[1,32,8]{1,2,0:T(8,128)} %bitcast.30), channel_id=1, replica_groups=mesh['expert'=16,'dp'=2] {'expert'}, dimensions={0}, use_global_device_ids=true | all-gather | bytes 17408 | tf_op jit(solution)/shard_map/all_gather | solution.py:15
  37.3 40.6 %all-gather.1 = f32[16,32,8]{1,2,0:T(8,128)S(1)} all-gather(f32[1,32,8]{1,2,0:T(8,128)} %bitcast.31), channel_id=1, replica_groups=mesh['expert'=16,'dp'=2] {'expert'}, dimensions={0}, use_global_device_ids=true | all-gather | bytes 17408 | tf_op jit(solution)/shard_map/all_gather | solution.py:16
  78.0 0.1 reshape.15
  78.1 5.1 %all-gather.5.cloned.1.call-done = bf16[512,3584]{1,0:T(8,128)(2,1)} async-done(((bf16[32,3584]{1,0:T(8,128)(2,1)}), bf16[512,3584]{1,0:T(8,128)(2,1)}) %all-gather.5.cloned.1.call-update) | async-done | bytes 3670032 | tf_op jit(solution)/shard_map/all_gather | solution.py:13
  83.2 0.0 copy-start
  83.2 9.3 %fusion.28 = bf16[512,1024]{1,0:T(8,128)(2,1)} fusion(bf16[512,3584]{1,0:T(8,128)(2,1)} %all-gather.5.cloned.1.call-done, bf16[1,3584,1024]{2,1,0:T(8,128)(2,1)} %param.11), kind=kOutput, calls=%fused_computation.31 | convolution fusion | flops 3758620672 | bytes 12058624 | tf_op jit(solution)/shard_map/dot_general | solution.py:20
  92.5 0.0 copy-done
  92.5 7.5 %fusion.31 = bf16[512,1024]{1,0:T(8,128)(2,1)} fusion(bf16[512,3584]{1,0:T(8,128)(2,1)S(1)} %copy-done, bf16[1,3584,1024]{2,1,0:T(8,128)(2,1)} %param.12), kind=kOutput, calls=%fused_computation.32 | convolution fusion | flops 3758620672 | bytes 12058624 | tf_op jit(solution)/shard_map/dot_general | solution.py:21
  100.0 56.2 %all-gather.7.cloned.1.call-done = bf16[512,3584]{1,0:T(8,128)(2,1)} async-done(((bf16[32,3584]{1,0:T(8,128)(2,1)}), bf16[512,3584]{1,0:T(8,128)(2,1)}) %all-gather.7.cloned.1.call-update) | async-done | bytes 3670032 | tf_op jit(solution)/shard_map/all_gather | solution.py:14
  156.2 9.2 %multiply_convert_fusion.1 = bf16[512,1024]{1,0:T(8,128)(2,1)} fusion(bf16[512,3584]{1,0:T(8,128)(2,1)} %all-gather.7.cloned.1.call-done, bf16[1,3584,1024]{2,1,0:T(8,128)(2,1)} %param.13, f32[512]{0:T(512)S(1)} %reshape.15), kind=kOutput, calls=%fused_computation.30 | convolution fusion | flops 3759144960 | bytes 12060672 | tf_op jit(solution)/shard_map/dot_general | solution.py:22
  165.4 0.0 all-reduce.3.cloned.1.call-update
  165.4 0.2 reduce-scatter.5.cloned.1.call-start
  165.7 0.1 reshape.12
  165.8 23.1 %all-reduce.3.cloned.1.call-done = (bf16[512,1024]{1,0:T(8,128)(2,1)}, bf16[512,1024]{1,0:T(8,128)(2,1)}, bf16[512,1024]{1,0:T(8,128)(2,1)}) async-done(((bf16[512,1024]{1,0:T(8,128)(2,1)}, bf16[512,1024]{1,0:T(8,128)(2,1)}, bf16[512,1024]{1,0:T(8,128)(2,1)}), (bf16[512,1024]{1,0:T(8,128)(2,1)}, bf16[512,1024]{1,0:T(8,128)(2,1)}, bf16[512,1024]{1,0:T(8,128)(2,1)})) %all-reduce.3.cloned.1.call-update) | async-done | bytes 3145744 | tf_op jit(solution)/shard_map/psum | solution.py:24
  188.8 0.0 copy-start.1
  188.8 0.0 copy-start.2
  188.8 0.0 copy-start.3
  188.8 10.9 %fusion.4 = f32[512,3584]{1,0:T(8,128)} fusion(bf16[1,3584,1024]{2,1,0:T(8,128)(2,1)} %param.12, bf16[512,1024]{1,0:T(8,128)(2,1)} %get-tuple-element.3, bf16[512,1024]{1,0:T(8,128)(2,1)} %get-tuple-element.4), kind=kOutput, calls=%fused_computation.4 | convolution fusion | flops 3762290688 | bytes 16777216 | tf_op jit(solution)/shard_map/dot_general | solution.py:34
  199.8 0.0 copy-done.1
  199.8 0.0 copy-done.2
  199.8 0.0 copy-done.3
  199.8 10.3 %select_convert_fusion = bf16[512,3584]{1,0:T(8,128)(2,1)} fusion(f32[512,3584]{1,0:T(8,128)} %fusion.4, bf16[1,3584,1024]{2,1,0:T(8,128)(2,1)} %param.11, pred[512]{0:T(512)(128)(4,1)S(1)} %reshape.12, bf16[512,1024]{1,0:T(8,128)(2,1)S(1)} %copy-done.1, bf16[512,1024]{1,0:T(8,128)(2,1)S(1)} %copy-done.3, bf16[512,1024]{1,0:T(8,128)(2,1)S(1)} %copy-done.2), kind=kOutput, calls=%fused_computation.12 | convolution fusion | flops 3770417152 | bytes 21496320 | tf_op jit(solution)/shard_map/dot_general | solution.py:33
  210.1 0.0 reduce-scatter.5.cloned.1.call-update
  210.1 0.0 reduce-scatter.3.cloned.1.call-start
  210.2 8.8 %multiply_convert_fusion = bf16[512,3584]{1,0:T(8,128)(2,1)} fusion(bf16[1,3584,1024]{2,1,0:T(8,128)(2,1)} %param.13, f32[512]{0:T(512)S(1)} %reshape.15, bf16[512,1024]{1,0:T(8,128)(2,1)S(1)} %copy-done.1, bf16[512,1024]{1,0:T(8,128)(2,1)S(1)} %copy-done.2), kind=kOutput, calls=%fused_computation.13 | convolution fusion | flops 3765960704 | bytes 13109248 | tf_op jit(solution)/shard_map/dot_general | solution.py:31
  218.9 0.0 reduce-scatter.3.cloned.1.call-update
  218.9 75.5 %reduce-scatter.5.cloned.1.call-done = bf16[32,3584]{1,0:T(8,128)(2,1)} async-done(((bf16[512,3584]{1,0:T(8,128)(2,1)}), bf16[32,3584]{1,0:T(8,128)(2,1)}) %reduce-scatter.5.cloned.1.call-update) | async-done | bytes 229392 | tf_op jit(solution)/shard_map/reduce_scatter | solution.py:38
  294.4 87.1 %reduce-scatter.3.cloned.1.call-done = bf16[32,3584]{1,0:T(8,128)(2,1)} async-done(((bf16[512,3584]{1,0:T(8,128)(2,1)}), bf16[32,3584]{1,0:T(8,128)(2,1)}) %reduce-scatter.3.cloned.1.call-update) | async-done | bytes 229392 | tf_op jit(solution)/shard_map/reduce_scatter | solution.py:37
  (2 shorter events, 0.1 us)
Async XLA Ops:
  7.2 76.1 %all-gather.5.cloned.1.call-start = ((), (), s32[]{:S(2)}) async-start(), calls=%async_computation.2 | async-start | bytes 3899392 | tf_op jit(solution)/shard_map/all_gather | solution.py:13
  7.9 148.4 %all-gather.7.cloned.1.call-start = ((), (), s32[]{:S(2)}) async-start(), calls=%async_computation.4 | async-start | bytes 3899392 | tf_op jit(solution)/shard_map/all_gather | solution.py:14
  8.6 180.2 %all-reduce.3.cloned.1.call-start = ((), (), s32[]{:S(2)}) async-start(), calls=%async_computation.6 | async-start | bytes 6291456 | tf_op jit(solution)/shard_map/psum | solution.py:24
  83.2 9.3 %copy-start = (bf16[512,3584]{1,0:T(8,128)(2,1)S(1)}, bf16[512,3584]{1,0:T(8,128)(2,1)}, u32[]{:S(2)}) copy-start(bf16[512,3584]{1,0:T(8,128)(2,1)} %all-gather.5.cloned.1.call-done) | copy-start | bytes 11010052
  165.4 129.0 %reduce-scatter.5.cloned.1.call-start = ((), (), s32[]{:S(2)}) async-start(), calls=%async_computation.5 | async-start | bytes 3899392 | tf_op jit(solution)/shard_map/reduce_scatter | solution.py:38
  188.8 10.9 %copy-start.1 = (bf16[512,1024]{1,0:T(8,128)(2,1)S(1)}, bf16[512,1024]{1,0:T(8,128)(2,1)}, u32[]{:S(2)}) copy-start(bf16[512,1024]{1,0:T(8,128)(2,1)} %get-tuple-element.2) | copy-start | bytes 3145732
  188.8 10.9 %copy-start.2 = (bf16[512,1024]{1,0:T(8,128)(2,1)S(1)}, bf16[512,1024]{1,0:T(8,128)(2,1)}, u32[]{:S(2)}) copy-start(bf16[512,1024]{1,0:T(8,128)(2,1)} %get-tuple-element.3) | copy-start | bytes 3145732
  188.8 10.9 %copy-start.3 = (bf16[512,1024]{1,0:T(8,128)(2,1)S(1)}, bf16[512,1024]{1,0:T(8,128)(2,1)}, u32[]{:S(2)}) copy-start(bf16[512,1024]{1,0:T(8,128)(2,1)} %get-tuple-element.4) | copy-start | bytes 3145732
  210.1 171.4 %reduce-scatter.3.cloned.1.call-start = ((), (), s32[]{:S(2)}) async-start(), calls=%async_computation.3 | async-start | bytes 3899392 | tf_op jit(solution)/shard_map/reduce_scatter | solution.py:37
Sparse Core Ops, SparseCore 0:
  10.7 72.4 all-gather.4
  86.0 70.2 all-gather.6
  165.6 23.2 all-reduce.2
  210.2 84.1 reduce-scatter.4
  297.1 84.3 reduce-scatter.2

commit v2 on v1

v2 whole, which is shorter than its diff:
```python
import jax
import jax.numpy as jnp
from jax import lax
from jax.experimental import pallas as pl
from jax.experimental.pallas import tpu as pltpu
from jax.sharding import PartitionSpec as P

F32, BF16 = jnp.float32, jnp.bfloat16
HERE, X, Y, XY = 0, 1, 2, 3
LANES = 128


class Grid:
    def __init__(self, size):
        assert size % 4 == 0
        self.rings = rings = size // 4
        self.size = size
        self.x = [(e, e ^ 1) for e in range(size)]
        self.y = [(e, e ^ 2) for e in range(size)]
        places = list(range(rings))
        cut = (rings + 1) // 2
        leaving = places[1:] + places[:1]
        self.leaving = [leaving[:cut], leaving[cut:]]

    def on(self, steps):
        return [(e, (e + 4 * steps) % self.size) for e in range(self.size)]


def send(value, pairs, axis="expert"):
    return lax.ppermute(value, axis, pairs)


def rows(*parts):
    return jnp.concatenate(parts, axis=0) if len(parts) > 1 else parts[0]


def around(grid, block):
    blocks = [block]
    for i in range(1, grid.rings):
        blocks.append(send(block, grid.on(i)))
    return blocks


def gather_by_place(grid, block):
    parts = []
    for p, here in enumerate(around(grid, block)):
        over_y = send(here, grid.y)
        over_x = send(here, grid.x)
        if p % 2:
            over_xy = send(over_y, grid.x)
        else:
            over_xy = send(over_x, grid.y)
        parts.append((here, over_x, over_y, over_xy))
    return parts


def gather_ring_first(grid, block):
    here = rows(*around(grid, block))
    over_x = send(here, grid.x)
    over_y = send(here, grid.y)
    over_xy = send(over_y, grid.x)
    return here, over_x, over_y, over_xy


def gather_ring_last(grid, block):
    over_y = send(block, grid.y)
    over_x = send(block, grid.x)
    over_xy = send(over_y, grid.x)
    return around(grid, rows(block, over_x, over_y, over_xy))


class Piece:
    def __init__(self, source, row, count, shift, width, first=0, column=0):
        self.source, self.row, self.count = source, row, count
        self.shift, self.width, self.first, self.column = shift, width, first, column


def fused_dot(arrays, pieces, height, width, weights, tail, scale):
    columns = weights[0].shape[1]
    step = 512
    per = columns // step
    count = len(arrays)
    masked = tail is not None
    tail_pieces = [
        Piece(p.source, p.row, p.count, 0, LANES, p.first, width) for p in pieces
    ] if masked else []
    moves = pieces + tail_pieces

    def kernel(*refs):
        sources = refs[:count]
        w_refs = refs[count : count + len(weights)]
        extra = refs[count + len(weights)]
        out = refs[count + len(weights) + 1]
        rest = refs[count + len(weights) + 2 :]
        if masked:
            sums, full, ends, sem = rest
        else:
            full, sem = rest
        at = pl.program_id(0)

        @pl.when(at == 0)
        def _():
            copies = []
            for i, p in enumerate(moves):
                target = full if i < len(pieces) else ends
                copies.append(
                    pltpu.make_async_copy(
                        sources[p.source].at[
                            pl.ds(p.first, p.count), pl.ds(p.column, p.width)
                        ],
                        target.at[pl.ds(p.row, p.count), pl.ds(p.shift, p.width)],
                        sem.at[i],
                    )
                )
            for c in copies:
                c.start()
            for c in copies:
                c.wait()
            if masked:
                value = ends[...].astype(F32) * extra[...]
                sums[...] = jnp.broadcast_to(
                    jnp.sum(value, axis=1, keepdims=True), sums.shape
                )

        for i, w in enumerate(w_refs):

            @pl.when(at // per == i)
            def _(w=w):
                part = jnp.dot(full[...], w[...], preferred_element_type=F32)
                if not masked:
                    part = part * extra[:, :1]
                out[...] = part.astype(BF16)

    weights = [pltpu.with_memory_space_constraint(w, pltpu.HBM) for w in weights]

    def w_map(i):
        return lambda at: (0, jnp.clip(at - i * per, 0, per - 1))

    extra = tail if masked else scale
    out_shape = [jax.ShapeDtypeStruct((height, columns * len(weights)), BF16)]
    out_specs = [pl.BlockSpec((height, step), lambda at: (0, at))]
    scratch = [pltpu.VMEM((height, width), BF16)]
    if masked:
        out_shape.append(jax.ShapeDtypeStruct((height, LANES), F32))
        out_specs.append(pl.BlockSpec((height, LANES), lambda at: (0, 0)))
        scratch.append(pltpu.VMEM((height, LANES), BF16))
    scratch.append(pltpu.SemaphoreType.DMA((len(moves),)))
    flops = 2 * height * width * columns * len(weights)
    moved = 2 * (width * columns * len(weights) + height * width + height * columns)
    return pl.pallas_call(
        kernel,
        grid=(per * len(weights),),
        in_specs=[pl.BlockSpec(memory_space=pl.ANY)] * count
        + [pl.BlockSpec((width, step), w_map(i)) for i in range(len(weights))]
        + [pl.BlockSpec(extra.shape, lambda at: (0, 0))],
        out_specs=out_specs,
        out_shape=out_shape,
        scratch_shapes=scratch,
        compiler_params=pltpu.CompilerParams(
            dimension_semantics=("arbitrary",), vmem_limit_bytes=26 << 20
        ),
        cost_estimate=pl.CostEstimate(flops=flops, bytes_accessed=moved, transcendentals=0),
    )(*arrays, *weights, extra)


def plus(value, got):
    return value.astype(F32) + got.astype(F32)


def scatter_around(grid, blocks):
    total = blocks[0]
    for i in range(1, grid.rings):
        total = plus(total, send(blocks[i].astype(BF16), grid.on(-i)))
    return total.astype(BF16)


def pairs(quarters, places):
    return [(q, p) for q in quarters for p in places]


def scatter_ring_last(grid, product):
    places = range(grid.rings)
    sent = product(pairs((XY, Y), places))
    got = send(sent, grid.y)
    total = plus(product(pairs((X, HERE), places)), got)
    size = total.shape[0] // 2
    got = send(total[:size].astype(BF16), grid.x)
    total = plus(total[size:], got)
    size //= grid.rings
    return scatter_around(grid, [total[p * size : (p + 1) * size] for p in places])


def scatter_ring_first(grid, product):
    blocks = {}
    for places in grid.leaving:
        part = product([(q, p) for p in places for q in (XY, X, Y, HERE)])
        size = part.shape[0] // max(1, len(places))
        for i, p in enumerate(places):
            blocks[p] = part[i * size : (i + 1) * size]
    plane = scatter_around(grid, blocks)
    size = plane.shape[0] // 4
    xy, x, y, here = [plane[q * size : (q + 1) * size] for q in range(4)]
    got = send(rows(xy, x), grid.x)
    over_y = plus(y, got[:size]).astype(BF16)
    here = plus(here, got[size:])
    got = send(over_y, grid.y)
    return plus(here, got).astype(BF16)


def scatter_two_ways(grid, product):
    groups = [g for g in grid.leaving if g]

    def split(value):
        size = value.shape[0] // grid.rings
        ends = [size * sum(len(h) for h in groups[:i]) for i in range(len(groups) + 1)]
        return [value[a:b] for a, b in zip(ends, ends[1:])]

    def part(quarters, side):
        return split(product([qp for g in groups for qp in pairs(quarters, g)], side))

    sent_left = part((XY, Y), 0)
    sent_right = part((XY, X), 1)
    got_left, got_right = [], []
    for g in range(len(groups)):
        got_left.append(send(sent_left[g], grid.y))
        got_right.append(send(sent_right[g], grid.x))
    kept_left = lax.optimization_barrier(part((X, HERE), 0))
    kept_right = lax.optimization_barrier(part((Y, HERE), 1))
    blocks = {}
    for g, places in enumerate(groups):
        left = plus(kept_left[g], got_left[g])
        right = plus(kept_right[g], got_right[g])
        size = left.shape[0] // 2
        over_x = send(left[:size].astype(BF16), grid.x)
        over_y = send(right[:size].astype(BF16), grid.y)
        total = jnp.concatenate([plus(left[size:], over_x), plus(right[size:], over_y)], axis=1)
        size //= len(places)
        for i, p in enumerate(places):
            blocks[p] = total[i * size : (i + 1) * size]
    return scatter_around(grid, blocks)


def native(tokens, cotangent, expert_ids, route_weight, gate_weight, up_weight, down_weight):
    me = lax.axis_index("expert")
    gate_w, up_w, down_w = gate_weight[0], up_weight[0], down_weight[0]
    all_tokens = lax.all_gather(tokens, "expert", axis=0, tiled=True)
    all_cot = lax.all_gather(cotangent, "expert", axis=0, tiled=True)
    all_ids = lax.all_gather(expert_ids, "expert", axis=0, tiled=True)
    all_weight = lax.all_gather(route_weight, "expert", axis=0, tiled=True)
    weight = jnp.sum(jnp.where(all_ids == me, all_weight, 0.0), axis=1, keepdims=True)
    gate_part = jnp.dot(all_tokens, gate_w, preferred_element_type=F32).astype(BF16)
    up_part = jnp.dot(all_tokens, up_w, preferred_element_type=F32).astype(BF16)
    grad_part = (weight * jnp.dot(all_cot, down_w, preferred_element_type=F32)).astype(BF16)
    gate = lax.psum(gate_part, "dp").astype(F32)
    up = lax.psum(up_part, "dp").astype(F32)
    hidden_grad = lax.psum(grad_part, "dp").astype(F32)
    sig = jax.nn.sigmoid(gate)
    hidden = (gate * sig * up).astype(BF16)
    up_grad = (hidden_grad * gate * sig).astype(BF16)
    gate_grad = (hidden_grad * up * sig * (1.0 + gate * (1.0 - sig))).astype(BF16)
    contract = (((1,), (1,)), ((), ()))
    out = lax.dot_general(hidden, down_w, contract, preferred_element_type=F32)
    grad = lax.dot_general(gate_grad, gate_w, contract, preferred_element_type=F32)
    grad += lax.dot_general(up_grad, up_w, contract, preferred_element_type=F32)
    return tuple(
        lax.psum_scatter(v.astype(BF16), "expert", scatter_dimension=0, tiled=True)
        for v in (weight * out, grad)
    )


def local(tokens, cotangent, expert_ids, route_weight, gate_weight, up_weight, down_weight):
    experts = lax.axis_size("expert")
    shares = lax.axis_size("dp")
    size, width = tokens.shape
    short = experts % 4 == 0 and experts // 4 <= 4 and 2 * experts <= LANES
    if not (short and shares == 2 and width % (2 * LANES) == 0 and size % 16 == 0):
        return native(
            tokens, cotangent, expert_ids, route_weight, gate_weight, up_weight, down_weight
        )
    grid = Grid(experts)
    me = lax.axis_index("expert")
    half = width // 2
    names = jnp.arange(experts, dtype=jnp.int32)
    named = expert_ids[:, :, None] == names[None, None, :]
    table = jnp.sum(jnp.where(named, route_weight[:, :, None], 0.0), axis=1)
    high = lax.reduce_precision(table, 8, 7)
    extra = jnp.concatenate([high, table - high], axis=1).astype(BF16)
    extra = jnp.pad(extra, ((0, 0), (0, -(2 * experts) % LANES)))
    block = jnp.concatenate([tokens, extra], axis=1)
    parts = gather_by_place(grid, block)
    by_quarter = gather_ring_first(grid, cotangent[:, :half])
    by_place = gather_ring_last(grid, cotangent[:, half:])
    gate_w = gate_weight[0]
    up_w = up_weight[0]
    down_w = down_weight[0]
    lanes = jnp.arange(extra.shape[1])[None, :]
    mine = ((lanes % experts) == me) & (lanes < 2 * experts)
    height = experts * size
    token_arrays, token_pieces = [], []
    cot_arrays = list(by_quarter) + by_place
    cot_pieces = []
    for q in range(4):
        cot_pieces.append(Piece(q, q * grid.rings * size, grid.rings * size, 0, half))
        for p in range(grid.rings):
            row = (q * grid.rings + p) * size
            token_pieces.append(Piece(len(token_arrays), row, size, 0, width))
            token_arrays.append(parts[p][q])
            cot_pieces.append(Piece(4 + p, row, size, half, width - half, q * size))

    def share_sum(part):
        return plus(part, send(part, [(0, 1), (1, 0)], "dp"))

    both, weight = fused_dot(
        token_arrays, token_pieces, height, width, [gate_w, up_w], mine.astype(F32), None
    )
    weight = weight[:, :1]
    both = share_sum(both)
    gate, up = both[:, : gate_w.shape[1]], both[:, gate_w.shape[1] :]
    sig = jax.nn.sigmoid(gate)
    hidden = (weight * (gate * sig * up)).astype(BF16)
    hidden, scale = lax.optimization_barrier((hidden, weight))
    (part,) = fused_dot(cot_arrays, cot_pieces, height, width, [down_w], None, scale)
    hidden_grad = share_sum(part)
    up_grad = (hidden_grad * gate * sig).astype(BF16)
    gate_grad = (hidden_grad * up * sig * (1.0 + gate * (1.0 - sig))).astype(BF16)
    contract = (((1,), (1,)), ((), ()))

    def rows_of(value, which):
        runs = []
        for q, p in which:
            start = (q * grid.rings + p) * size
            if runs and runs[-1][1] == start:
                runs[-1][1] = start + size
            else:
                runs.append([start, start + size])
        return rows(*[value[a:b] for a, b in runs])

    def back(value, w, which, side):
        return lax.dot_general(
            rows_of(value, which), w[side * half : (side + 1) * half], contract,
            preferred_element_type=F32,
        )

    def out_part(which, side):
        return back(hidden, down_w, which, side).astype(BF16)

    def grad_part(which, side):
        total = back(gate_grad, gate_w, which, side) + back(up_grad, up_w, which, side)
        return total.astype(BF16)

    mixed = jnp.concatenate(
        [
            scatter_ring_last(grid, lambda which: out_part(which, 0)),
            scatter_ring_first(grid, lambda which: out_part(which, 1)),
        ],
        axis=1,
    )
    grad_tokens = scatter_two_ways(grid, grad_part)
    return (mixed, grad_tokens)


def solution(mesh):
    return jax.shard_map(
        local,
        mesh=mesh,
        in_specs=(
            P("expert", "dp"),
            P("expert", "dp"),
            P("expert", None),
            P("expert", None),
            P("expert", "dp", None),
            P("expert", "dp", None),
            P("expert", "dp", None),
        ),
        out_specs=(P("expert", "dp"), P("expert", "dp")),
        check_vma=False,
    )
```

time: 393 us -> 252 us (0.64); the launches traced: 388 us -> 251 us
  waiting for transfers between devices: 248 us -> 155 us
  blocking collectives: 69.3 us -> 0 us
  starting transfers between devices: 0.38 us -> 47.6 us
  matrix products: 56 us -> 14.2 us
  Pallas kernels: 0 us -> 22 us
  between operations: 13.8 us -> 1.44 us
  other arithmetic: 0.07 us -> 7 us
  local copies, waits for them, and re-layouts: 0.18 us -> 4.53 us
    reduce_scatter x2 -> x0, waiting for transfers between devices: 163 us -> none  [the longest x1 87.1 us: local(): mixed = lax.psum_scatter(out, 'expert', scatter_dimension=0, tiled=True)]
    ppermute x0 -> x50, waiting for transfers between devices: none -> 155 us  [send(): return lax.ppermute(value, axis, pairs)]
    all_gather x2 -> x0, blocking collectives: 69.3 us -> none  [the longest x1 40.6 us: local(): all_weight = lax.all_gather(route_weight, 'expert', axis=0, tiled=True)]
    all_gather x2 -> x0, waiting for transfers between devices: 61.3 us -> none  [the longest x1 56.2 us: local(): all_cot = lax.all_gather(cotangent, 'expert', axis=0, tiled=True)]
    ppermute x0 -> x50, starting transfers between devices: none -> 47.6 us  [send(): return lax.ppermute(value, axis, pairs)]
    dot_general x6 -> x12, matrix products: 56 us -> 14.2 us  [back(): lax.dot_general(rows_of(value, which), w[side * half:(side + 1) * half],...]
    psum x1 -> x0, waiting for transfers between devices: 23.1 us -> none  [local(): up = lax.psum(up_part, 'dp').astype(f32)]
    pallas_call x0 -> x2, Pallas kernels: none -> 22 us  [fused_dot(): pl.pallas_call(kernel, grid=(per * len(weights),), in_specs=[pl.BlockSpec...]
  transfers between devices with their start and end apart: 5 -> 50, of which waited for: 5 -> 29; matrix products, arithmetic and copies ran while one was open for 7% -> 8% of each run, Pallas kernels for 0% -> 3%
where the time goes in v2:
time: 252 us; the launch traced here: 251 us
  waiting for transfers between devices  155 us (62%)
  starting transfers between devices  47.6 us (19%)
  Pallas kernels  22 us (9%)
  matrix products  14.2 us (6%)
  other arithmetic  7 us (3%)
  local copies, waits for them, and re-layouts  4.53 us (2%)
    ppermute x50, waiting for transfers between devices, send(): return lax.ppermute(value, axis, pairs)  155 us
    ppermute x50, starting transfers between devices, send(): return lax.ppermute(value, axis, pairs)  47.6 us
    pallas_call x2, Pallas kernels, fused_dot(): pl.pallas_call(kernel, grid=(per * len(weights),), in_specs=[pl.BlockSpec...  22 us
    dot_general x12, matrix products, back(): lax.dot_general(rows_of(value, which), w[side * half:(side + 1) * half],...  14.2 us
  transfers between devices with their start and end apart: 50, of which 29 were waited for; matrix products, arithmetic and copies ran while one was open for 8% of the time, Pallas kernels for 3%

profile of v2, /device:TPU:14, one launch (start us, length us, event | category | flops | bytes accessed | tf_op | source)
XLA Modules:
  0.0 251.3 jit_solution(4676200192541318440)
XLA Ops:
  2.6 1.6 collective-permute-start
  4.2 1.2 collective-permute-start.1
  5.4 1.8 collective-permute-start.2
  8.3 12.3 %collective-permute-done.refs_1_ = bf16[32,3712]{1,0:T(8,128)(2,1)S(1)} collective-permute-done((bf16[32,3712]{1,0:T(8,128)(2,1)S(1)}, bf16[32,3712]{1,0:T(8,128)(2,1)S(1)}, u32[]{:S(2)}, u32[]{:S(2)}) %collective-permute-start) | collective-permute-done | bytes 237600 | tf_op jit(solution)/shard_map/ppermute | solution.py:30
  21.1 3.4 %collective-permute-done.1.refs_2_ = bf16[32,3712]{1,0:T(8,128)(2,1)S(1)} collective-permute-done((bf16[32,3712]{1,0:T(8,128)(2,1)S(1)}, bf16[32,3712]{1,0:T(8,128)(2,1)S(1)}, u32[]{:S(2)}, u32[]{:S(2)}) %collective-permute-start.1) | collective-permute-done | bytes 237600 | tf_op jit(solution)/shard_map/ppermute | solution.py:30
  25.0 1.3 collective-permute-done.2.refs_3_
  27.4 1.5 collective-permute-start.10
  29.4 3.8 %collective-permute-done.5.refs_6_ = bf16[32,3712]{1,0:T(8,128)(2,1)S(1)} collective-permute-done((bf16[32,3712]{1,0:T(8,128)(2,1)S(1)}, bf16[32,3712]{1,0:T(8,128)(2,1)S(1)}, u32[]{:S(2)}, u32[]{:S(2)}) %collective-permute-start.5) | collective-permute-done | bytes 237600 | tf_op jit(solution)/shard_map/ppermute | solution.py:30
  33.7 1.3 collective-permute-done.8.refs_9_
  35.5 2.4 collective-permute-done.6.refs_7_
  38.4 1.6 collective-permute-done.10.refs_11_
  40.6 4.5 %collective-permute-done.9.refs_10_ = bf16[32,3712]{1,0:T(8,128)(2,1)S(1)} collective-permute-done((bf16[32,3712]{1,0:T(8,128)(2,1)S(1)}, bf16[32,3712]{1,0:T(8,128)(2,1)S(1)}, u32[]{:S(2)}, u32[]{:S(2)}) %collective-permute-start.9) | collective-permute-done | bytes 237600 | tf_op jit(solution)/shard_map/ppermute | solution.py:30
  45.1 5.1 %collective-permute-done.11.refs_12_ = bf16[32,3712]{1,0:T(8,128)(2,1)S(1)} collective-permute-done((bf16[32,3712]{1,0:T(8,128)(2,1)S(1)}, bf16[32,3712]{1,0:T(8,128)(2,1)S(1)}, u32[]{:S(2)}, u32[]{:S(2)}) %collective-permute-start.11) | collective-permute-done | bytes 237600 | tf_op jit(solution)/shard_map/ppermute | solution.py:30
  50.2 4.2 %collective-permute-done.13.refs_14_ = bf16[32,3712]{1,0:T(8,128)(2,1)} collective-permute-done((bf16[32,3712]{1,0:T(8,128)(2,1)S(1)}, bf16[32,3712]{1,0:T(8,128)(2,1)}, u32[]{:S(2)}, u32[]{:S(2)}) %collective-permute-start.13) | collective-permute-done | bytes 237600 | tf_op jit(solution)/shard_map/ppermute | solution.py:30
  54.5 14.4 %shard_map.86 = (bf16[512,2048]{1,0:T(8,128)(2,1)S(1)}, f32[512,128]{1,0:T(8,128)S(1)}) custom-call(bf16[32,3712]{1,0:T(8,128)(2,1)S(1)} %pad_maximum_fusion.3.refs_0_, bf16[32,3712]{1,0:T(8,128)(2,1)S(1)} %collective-permute-done.refs_1_, bf16[32,3712]{1,0:T(8,128)(2,1)S(1)} %collective-permute-done.1.refs_2_, ...), custom_call_target="tpu_custom_call" | custom-call | flops 7516192768 | bytes 19398656 | tf_op jit(solution)/shard_map/pallas_call | solution.py:150
  70.6 2.7 %collective-permute-start.26 = (bf16[32,1792]{1,0:T(8,128)(2,1)S(1)}, bf16[32,1792]{1,0:T(8,128)(2,1)S(1)}, u32[]{:S(2)}, u32[]{:S(2)}) collective-permute-start(bf16[32,1792]{1,0:T(8,128)(2,1)S(1)} %get-tuple-element.100), channel_id=1, source_target_pairs={{0,8},{2,10},{4,12},{6,14},{8,16},{10,18},{12,20},{14,22},{16,24},... | collective-permute-start | bytes 344072 | tf_op jit(solution)/shard_map/ppermute | solution.py:30
  73.3 6.7 %collective-permute-done.28 = bf16[32,1792]{1,0:T(8,128)(2,1)S(1)} collective-permute-done((bf16[32,1792]{1,0:T(8,128)(2,1)S(1)}, bf16[32,1792]{1,0:T(8,128)(2,1)S(1)}, u32[]{:S(2)}, u32[]{:S(2)}) %collective-permute-start.28) | collective-permute-done | bytes 114720 | tf_op jit(solution)/shard_map/ppermute | solution.py:30
  80.0 2.0 collective-permute-start.34
  82.2 1.1 collective-permute-start.30
  83.3 2.7 %collective-permute-done.32 = bf16[32,1792]{1,0:T(8,128)(2,1)S(1)} collective-permute-done((bf16[32,1792]{1,0:T(8,128)(2,1)S(1)}, bf16[32,1792]{1,0:T(8,128)(2,1)S(1)}, u32[]{:S(2)}, u32[]{:S(2)}) %collective-permute-start.32) | collective-permute-done | bytes 114720 | tf_op jit(solution)/shard_map/ppermute | solution.py:30
  86.0 2.5 collective-permute-done.34
  91.7 1.2 fusion.57
  93.0 1.2 fusion.60
  94.3 2.1 collective-permute-start.21
  96.5 1.2 fusion.54
  97.7 1.5 collective-permute-start.35
  99.1 22.5 %collective-permute-done.23 = bf16[128,1792]{1,0:T(8,128)(2,1)S(1)} collective-permute-done((bf16[128,1792]{1,0:T(8,128)(2,1)S(1)}, bf16[128,1792]{1,0:T(8,128)(2,1)S(1)}, u32[]{:S(2)}, u32[]{:S(2)}) %collective-permute-start.23) | collective-permute-done | bytes 458784 | tf_op jit(solution)/shard_map/ppermute | solution.py:30
  121.6 26.6 %collective-permute-done.22 = bf16[128,1792]{1,0:T(8,128)(2,1)S(1)} collective-permute-done((bf16[128,1792]{1,0:T(8,128)(2,1)S(1)}, bf16[128,1792]{1,0:T(8,128)(2,1)S(1)}, u32[]{:S(2)}, u32[]{:S(2)}) %collective-permute-start.22) | collective-permute-done | bytes 458784 | tf_op jit(solution)/shard_map/ppermute | solution.py:30
  148.2 2.5 collective-permute-done.21
  150.6 1.4 collective-permute-start.31
  152.3 1.2 collective-permute-start.16
  153.6 9.3 %collective-permute-done.35.refs_5_ = bf16[128,1792]{1,0:T(8,128)(2,1)S(1)} collective-permute-done((bf16[128,1792]{1,0:T(8,128)(2,1)S(1)}, bf16[128,1792]{1,0:T(8,128)(2,1)S(1)}, u32[]{:S(2)}, u32[]{:S(2)}) %collective-permute-start.35) | collective-permute-done | bytes 458784 | tf_op jit(solution)/shard_map/ppermute | solution.py:30
  162.9 5.7 %collective-permute-done.36.refs_6_ = bf16[128,1792]{1,0:T(8,128)(2,1)S(1)} collective-permute-done((bf16[128,1792]{1,0:T(8,128)(2,1)S(1)}, bf16[128,1792]{1,0:T(8,128)(2,1)S(1)}, u32[]{:S(2)}, u32[]{:S(2)}) %collective-permute-start.36) | collective-permute-done | bytes 458784 | tf_op jit(solution)/shard_map/ppermute | solution.py:30
  168.6 1.7 collective-permute-done.37.refs_7_
  170.2 7.6 %shard_map.87 = bf16[512,1024]{1,0:T(8,128)(2,1)S(1)} custom-call(bf16[128,1792]{1,0:T(8,128)(2,1)S(1)} %pad_maximum_fusion.1.refs_0_, bf16[128,1792]{1,0:T(8,128)(2,1)S(1)} %collective-permute-done.29.refs_1_, bf16[128,1792]{1,0:T(8,128)(2,1)S(1)} %collective-permute-done.30.refs_2_, bf16[128,1792]{1,0:T(8,128)(2,1)S(1)} %collective-permute-done.31.refs_3_, ...), custom_call_target="tpu_custom_call" | custom-call | flops 3758096384 | bytes 12058624 | tf_op jit(solution)/shard_map/pallas_call | solution.py:150
  177.9 1.5 collective-permute-start.25
  179.5 4.1 %collective-permute-done.25 = bf16[32,1792]{1,0:T(8,128)(2,1)S(1)} collective-permute-done((bf16[32,1792]{1,0:T(8,128)(2,1)S(1)}, bf16[32,1792]{1,0:T(8,128)(2,1)S(1)}, u32[]{:S(2)}, u32[]{:S(2)}) %collective-permute-start.25) | collective-permute-done | bytes 114720 | tf_op jit(solution)/shard_map/ppermute | solution.py:30
  183.6 1.2 convert_add_fusion.2
  184.9 1.5 collective-permute-start.17
  186.4 1.2 multiply_convert_fusion.1
  187.9 1.2 fusion.8
  190.0 1.0 slice-done.7
  191.0 1.2 fusion.69
  192.3 1.2 collective-permute-start.39
  193.5 1.2 fusion.10
  194.7 1.2 fusion.72
  196.0 1.2 fusion
  197.2 1.2 fusion.63
  199.4 1.2 fusion.2
  200.6 1.2 fusion.66
  202.7 1.9 collective-permute-start.18
  204.7 3.4 %collective-permute-done.20 = bf16[32,1792]{1,0:T(8,128)(2,1)S(1)} collective-permute-done((bf16[32,1792]{1,0:T(8,128)(2,1)S(1)}, bf16[32,1792]{1,0:T(8,128)(2,1)S(1)}, u32[]{:S(2)}, u32[]{:S(2)}) %collective-permute-start.20) | collective-permute-done | bytes 114720 | tf_op jit(solution)/shard_map/ppermute | solution.py:30
  208.1 1.1 collective-permute-start.45
  209.2 1.8 collective-permute-done.19
  212.9 1.0 collective-permute-start.40
  214.1 1.4 collective-permute-start.42
  215.5 6.3 %collective-permute-done.45 = bf16[128,1792]{1,0:T(8,128)(2,1)S(1)} collective-permute-done((bf16[128,1792]{1,0:T(8,128)(2,1)S(1)}, bf16[128,1792]{1,0:T(8,128)(2,1)S(1)}, u32[]{:S(2)}, u32[]{:S(2)}) %collective-permute-start.45) | collective-permute-done | bytes 458784 | tf_op jit(solution)/shard_map/ppermute | solution.py:30
  223.9 2.7 %collective-permute-done.40 = bf16[64,1792]{1,0:T(8,128)(2,1)S(1)} collective-permute-done((bf16[64,1792]{1,0:T(8,128)(2,1)S(1)}, bf16[64,1792]{1,0:T(8,128)(2,1)S(1)}, u32[]{:S(2)}, u32[]{:S(2)}) %collective-permute-start.40) | collective-permute-done | bytes 229408 | tf_op jit(solution)/shard_map/ppermute | solution.py:30
  226.9 2.7 %collective-permute-start.49 = (bf16[32,3584]{1,0:T(8,128)(2,1)S(1)}, bf16[32,3584]{1,0:T(8,128)(2,1)S(1)}, u32[]{:S(2)}, u32[]{:S(2)}) collective-permute-start(bf16[32,3584]{1,0:T(8,128)(2,1)S(1)} %fusion.90), channel_id=1, source_target_pairs={{0,8},{2,10},{4,12},{6,14},{8,16},{10,18},{12,20},{14,22},{16,24},... | collective-permute-start | bytes 688136 | tf_op jit(solution)/shard_map/ppermute | solution.py:30
  229.8 3.2 %collective-permute-start.48 = (bf16[32,3584]{1,0:T(8,128)(2,1)S(1)}, bf16[32,3584]{1,0:T(8,128)(2,1)S(1)}, u32[]{:S(2)}, u32[]{:S(2)}) collective-permute-start(bf16[32,3584]{1,0:T(8,128)(2,1)S(1)} %get-tuple-element.93), channel_id=1, source_target_pairs={{0,16},{2,18},{4,20},{6,22},{8,24},{10,26},{12,28},{14,30},{16,0},... | collective-permute-start | bytes 688136 | tf_op jit(solution)/shard_map/ppermute | solution.py:30
  233.0 1.6 collective-permute-start.47
  235.3 9.7 %collective-permute-done.49 = bf16[32,3584]{1,0:T(8,128)(2,1)S(1)} collective-permute-done((bf16[32,3584]{1,0:T(8,128)(2,1)S(1)}, bf16[32,3584]{1,0:T(8,128)(2,1)S(1)}, u32[]{:S(2)}, u32[]{:S(2)}) %collective-permute-start.49) | collective-permute-done | bytes 229408 | tf_op jit(solution)/shard_map/ppermute | solution.py:30
  245.1 2.5 collective-permute-done.48
  247.5 3.0 %collective-permute-done.47 = bf16[32,3584]{1,0:T(8,128)(2,1)S(1)} collective-permute-done((bf16[32,3584]{1,0:T(8,128)(2,1)S(1)}, bf16[32,3584]{1,0:T(8,128)(2,1)S(1)}, u32[]{:S(2)}, u32[]{:S(2)}) %collective-permute-start.47) | collective-permute-done | bytes 229408 | tf_op jit(solution)/shard_map/ppermute | solution.py:30
  (146 shorter events, 22.5 us)
Async XLA Ops:
  2.6 18.0 %collective-permute-start = (bf16[32,3712]{1,0:T(8,128)(2,1)S(1)}, bf16[32,3712]{1,0:T(8,128)(2,1)S(1)}, u32[]{:S(2)}, u32[]{:S(2)}) collective-permute-start(bf16[32,3712]{1,0:T(8,128)(2,1)S(1)} %pad_maximum_fusion.3.refs_0_), channel_id=1, source_target_pairs={{0,8},{2,10},{4,12},{6,14},{8,16},{10,18},{12,20},{14,22},{16,24},... | collective-permute-start | bytes 712712 | tf_op jit(solution)/shard_map/ppermute | solution.py:30
  4.2 20.3 %collective-permute-start.1 = (bf16[32,3712]{1,0:T(8,128)(2,1)S(1)}, bf16[32,3712]{1,0:T(8,128)(2,1)S(1)}, u32[]{:S(2)}, u32[]{:S(2)}) collective-permute-start(bf16[32,3712]{1,0:T(8,128)(2,1)S(1)} %pad_maximum_fusion.3.refs_0_), channel_id=1, source_target_pairs={{0,16},{2,18},{4,20},{6,22},{8,24},{10,26},{12,28},{14,30},{16,0},... | collective-permute-start | bytes 712712 | tf_op jit(solution)/shard_map/ppermute | solution.py:30
  5.4 20.9 %collective-permute-start.2 = (bf16[32,3712]{1,0:T(8,128)(2,1)S(1)}, bf16[32,3712]{1,0:T(8,128)(2,1)S(1)}, u32[]{:S(2)}, u32[]{:S(2)}) collective-permute-start(bf16[32,3712]{1,0:T(8,128)(2,1)S(1)} %pad_maximum_fusion.3.refs_0_), channel_id=1, source_target_pairs={{0,24},{2,26},{4,28},{6,30},{8,0},{10,2},{12,4},{14,6},{16,8},{18,... | collective-permute-start | bytes 712712 | tf_op jit(solution)/shard_map/ppermute | solution.py:30
  7.2 19.6 %collective-permute-start.3 = (bf16[32,3712]{1,0:T(8,128)(2,1)S(1)}, bf16[32,3712]{1,0:T(8,128)(2,1)S(1)}, u32[]{:S(2)}, u32[]{:S(2)}) collective-permute-start(bf16[32,3712]{1,0:T(8,128)(2,1)S(1)} %pad_maximum_fusion.3.refs_0_), channel_id=1, source_target_pairs={{0,2},{2,0},{4,6},{6,4},{8,10},{10,8},{12,14},{14,12},{16,18},{18,... | collective-permute-start | bytes 712712 | tf_op jit(solution)/shard_map/ppermute | solution.py:30
  7.8 19.6 %collective-permute-start.7 = (bf16[32,3712]{1,0:T(8,128)(2,1)S(1)}, bf16[32,3712]{1,0:T(8,128)(2,1)S(1)}, u32[]{:S(2)}, u32[]{:S(2)}) collective-permute-start(bf16[32,3712]{1,0:T(8,128)(2,1)S(1)} %pad_maximum_fusion.3.refs_0_), channel_id=1, source_target_pairs={{0,4},{2,6},{4,0},{6,2},{8,12},{10,14},{12,8},{14,10},{16,20},{18,... | collective-permute-start | bytes 712712 | tf_op jit(solution)/shard_map/ppermute | solution.py:30
  20.5 8.3 %collective-permute-start.4 = (bf16[32,3712]{1,0:T(8,128)(2,1)S(1)}, bf16[32,3712]{1,0:T(8,128)(2,1)S(1)}, u32[]{:S(2)}, u32[]{:S(2)}) collective-permute-start(bf16[32,3712]{1,0:T(8,128)(2,1)S(1)} %collective-permute-done.refs_1_), channel_id=1, source_target_pairs={{0,2},{2,0},{4,6},{6,4},{8,10},{10,8},{12,14},{14,12},{16,18},{18,... | collective-permute-start | bytes 712712 | tf_op jit(solution)/shard_map/ppermute | solution.py:30
  24.5 8.6 %collective-permute-start.5 = (bf16[32,3712]{1,0:T(8,128)(2,1)S(1)}, bf16[32,3712]{1,0:T(8,128)(2,1)S(1)}, u32[]{:S(2)}, u32[]{:S(2)}) collective-permute-start(bf16[32,3712]{1,0:T(8,128)(2,1)S(1)} %collective-permute-done.1.refs_2_), channel_id=1, source_target_pairs={{0,2},{2,0},{4,6},{6,4},{8,10},{10,8},{12,14},{14,12},{16,18},{18,... | collective-permute-start | bytes 712712 | tf_op jit(solution)/shard_map/ppermute | solution.py:30
  26.3 8.7 %collective-permute-start.8 = (bf16[32,3712]{1,0:T(8,128)(2,1)S(1)}, bf16[32,3712]{1,0:T(8,128)(2,1)S(1)}, u32[]{:S(2)}, u32[]{:S(2)}) collective-permute-start(bf16[32,3712]{1,0:T(8,128)(2,1)S(1)} %collective-permute-done.refs_1_), channel_id=1, source_target_pairs={{0,4},{2,6},{4,0},{6,2},{8,12},{10,14},{12,8},{14,10},{16,20},{18,... | collective-permute-start | bytes 712712 | tf_op jit(solution)/shard_map/ppermute | solution.py:30
  26.8 11.1 %collective-permute-start.6 = (bf16[32,3712]{1,0:T(8,128)(2,1)S(1)}, bf16[32,3712]{1,0:T(8,128)(2,1)S(1)}, u32[]{:S(2)}, u32[]{:S(2)}) collective-permute-start(bf16[32,3712]{1,0:T(8,128)(2,1)S(1)} %collective-permute-done.2.refs_3_), channel_id=1, source_target_pairs={{0,2},{2,0},{4,6},{6,4},{8,10},{10,8},{12,14},{14,12},{16,18},{18,... | collective-permute-start | bytes 712712 | tf_op jit(solution)/shard_map/ppermute | solution.py:30
  27.4 12.7 %collective-permute-start.10 = (bf16[32,3712]{1,0:T(8,128)(2,1)S(1)}, bf16[32,3712]{1,0:T(8,128)(2,1)S(1)}, u32[]{:S(2)}, u32[]{:S(2)}) collective-permute-start(bf16[32,3712]{1,0:T(8,128)(2,1)S(1)} %collective-permute-done.2.refs_3_), channel_id=1, source_target_pairs={{0,4},{2,6},{4,0},{6,2},{8,12},{10,14},{12,8},{14,10},{16,20},{18,... | collective-permute-start | bytes 712712 | tf_op jit(solution)/shard_map/ppermute | solution.py:30
  28.9 16.3 %collective-permute-start.9 = (bf16[32,3712]{1,0:T(8,128)(2,1)S(1)}, bf16[32,3712]{1,0:T(8,128)(2,1)S(1)}, u32[]{:S(2)}, u32[]{:S(2)}) collective-permute-start(bf16[32,3712]{1,0:T(8,128)(2,1)S(1)} %collective-permute-done.1.refs_2_), channel_id=1, source_target_pairs={{0,4},{2,6},{4,0},{6,2},{8,12},{10,14},{12,8},{14,10},{16,20},{18,... | collective-permute-start | bytes 712712 | tf_op jit(solution)/shard_map/ppermute | solution.py:30
  33.2 17.1 %collective-permute-start.11 = (bf16[32,3712]{1,0:T(8,128)(2,1)S(1)}, bf16[32,3712]{1,0:T(8,128)(2,1)S(1)}, u32[]{:S(2)}, u32[]{:S(2)}) collective-permute-start(bf16[32,3712]{1,0:T(8,128)(2,1)S(1)} %collective-permute-done.3.refs_4_), channel_id=1, source_target_pairs={{0,4},{2,6},{4,0},{6,2},{8,12},{10,14},{12,8},{14,10},{16,20},{18,... | collective-permute-start | bytes 712712 | tf_op jit(solution)/shard_map/ppermute | solution.py:30
  35.0 15.3 %collective-permute-start.12 = (bf16[32,3712]{1,0:T(8,128)(2,1)S(1)}, bf16[32,3712]{1,0:T(8,128)(2,1)S(1)}, u32[]{:S(2)}, u32[]{:S(2)}) collective-permute-start(bf16[32,3712]{1,0:T(8,128)(2,1)S(1)} %collective-permute-done.8.refs_9_), channel_id=1, source_target_pairs={{0,2},{2,0},{4,6},{6,4},{8,10},{10,8},{12,14},{14,12},{16,18},{18,... | collective-permute-start | bytes 712712 | tf_op jit(solution)/shard_map/ppermute | solution.py:30
  37.9 16.6 %collective-permute-start.13 = (bf16[32,3712]{1,0:T(8,128)(2,1)S(1)}, bf16[32,3712]{1,0:T(8,128)(2,1)}, u32[]{:S(2)}, u32[]{:S(2)}) collective-permute-start(bf16[32,3712]{1,0:T(8,128)(2,1)S(1)} %collective-permute-done.5.refs_6_), channel_id=1, source_target_pairs={{0,4},{2,6},{4,0},{6,2},{8,12},{10,14},{12,8},{14,10},{16,20},{18,... | collective-permute-start | bytes 712712 | tf_op jit(solution)/shard_map/ppermute | solution.py:30
  40.0 14.4 %collective-permute-start.14 = (bf16[32,3712]{1,0:T(8,128)(2,1)S(1)}, bf16[32,3712]{1,0:T(8,128)(2,1)}, u32[]{:S(2)}, u32[]{:S(2)}) collective-permute-start(bf16[32,3712]{1,0:T(8,128)(2,1)S(1)} %collective-permute-done.10.refs_11_), channel_id=1, source_target_pairs={{0,2},{2,0},{4,6},{6,4},{8,10},{10,8},{12,14},{14,12},{16,18},{18,... | collective-permute-start | bytes 712712 | tf_op jit(solution)/shard_map/ppermute | solution.py:30
  54.5 14.5 %copy-start = (bf16[32,3584]{1,0:T(8,128)(2,1)S(1)}, bf16[32,3584]{1,0:T(8,128)(2,1)}, u32[]{:S(2)}) copy-start(bf16[32,3584]{1,0:T(8,128)(2,1)} %param.8) | copy-start | bytes 688132
  68.9 19.8 %collective-permute-start.15 = (bf16[512,2048]{1,0:T(8,128)(2,1)S(1)}, bf16[512,2048]{1,0:T(8,128)(2,1)S(1)}, u32[]{:S(2)}, u32[]{:S(2)}) collective-permute-start(bf16[512,2048]{1,0:T(8,128)(2,1)S(1)} %get-tuple-element.11), channel_id=1, source_target_pairs={{0,1},{1,0},{2,3},{3,2},{4,5},{5,4},{6,7},{7,6},{8,9},{9,8},{10,11... | collective-permute-start | bytes 6291464 | tf_op jit(solution)/shard_map/ppermute | solution.py:30
  69.0 11.0 %collective-permute-start.28 = (bf16[32,1792]{1,0:T(8,128)(2,1)S(1)}, bf16[32,1792]{1,0:T(8,128)(2,1)S(1)}, u32[]{:S(2)}, u32[]{:S(2)}) collective-permute-start(bf16[32,1792]{1,0:T(8,128)(2,1)S(1)} %get-tuple-element.100), channel_id=1, source_target_pairs={{0,24},{2,26},{4,28},{6,30},{8,0},{10,2},{12,4},{14,6},{16,8},{18,... | collective-permute-start | bytes 344072 | tf_op jit(solution)/shard_map/ppermute | solution.py:30
  69.1 10.9 %collective-permute-start.33 = (bf16[32,1792]{1,0:T(8,128)(2,1)S(1)}, bf16[32,1792]{1,0:T(8,128)(2,1)S(1)}, u32[]{:S(2)}, u32[]{:S(2)}) collective-permute-start(bf16[32,1792]{1,0:T(8,128)(2,1)S(1)} %get-tuple-element.99), channel_id=1, source_target_pairs={{0,4},{2,6},{4,0},{6,2},{8,12},{10,14},{12,8},{14,10},{16,20},{18,... | collective-permute-start | bytes 344072 | tf_op jit(solution)/shard_map/ppermute | solution.py:30
  69.7 12.4 %collective-permute-start.27 = (bf16[32,1792]{1,0:T(8,128)(2,1)S(1)}, bf16[32,1792]{1,0:T(8,128)(2,1)S(1)}, u32[]{:S(2)}, u32[]{:S(2)}) collective-permute-start(bf16[32,1792]{1,0:T(8,128)(2,1)S(1)} %get-tuple-element.100), channel_id=1, source_target_pairs={{0,16},{2,18},{4,20},{6,22},{8,24},{10,26},{12,28},{14,30},{16,0},... | collective-permute-start | bytes 344072 | tf_op jit(solution)/shard_map/ppermute | solution.py:30
  70.6 11.5 %collective-permute-start.26 = (bf16[32,1792]{1,0:T(8,128)(2,1)S(1)}, bf16[32,1792]{1,0:T(8,128)(2,1)S(1)}, u32[]{:S(2)}, u32[]{:S(2)}) collective-permute-start(bf16[32,1792]{1,0:T(8,128)(2,1)S(1)} %get-tuple-element.100), channel_id=1, source_target_pairs={{0,8},{2,10},{4,12},{6,14},{8,16},{10,18},{12,20},{14,22},{16,24},... | collective-permute-start | bytes 344072 | tf_op jit(solution)/shard_map/ppermute | solution.py:30
  80.0 6.0 %collective-permute-start.32 = (bf16[32,1792]{1,0:T(8,128)(2,1)S(1)}, bf16[32,1792]{1,0:T(8,128)(2,1)S(1)}, u32[]{:S(2)}, u32[]{:S(2)}) collective-permute-start(bf16[32,1792]{1,0:T(8,128)(2,1)S(1)} %get-tuple-element.99), channel_id=1, source_target_pairs={{0,2},{2,0},{4,6},{6,4},{8,10},{10,8},{12,14},{14,12},{16,18},{18,... | collective-permute-start | bytes 344072 | tf_op jit(solution)/shard_map/ppermute | solution.py:30
  80.0 8.5 %collective-permute-start.34 = (bf16[32,1792]{1,0:T(8,128)(2,1)S(1)}, bf16[32,1792]{1,0:T(8,128)(2,1)S(1)}, u32[]{:S(2)}, u32[]{:S(2)}) collective-permute-start(bf16[32,1792]{1,0:T(8,128)(2,1)S(1)} %collective-permute-done.33), channel_id=1, source_target_pairs={{0,2},{2,0},{4,6},{6,4},{8,10},{10,8},{12,14},{14,12},{16,18},{18,... | collective-permute-start | bytes 344072 | tf_op jit(solution)/shard_map/ppermute | solution.py:30
  82.1 70.2 %collective-permute-start.29 = (bf16[128,1792]{1,0:T(8,128)(2,1)S(1)}, bf16[128,1792]{1,0:T(8,128)(2,1)S(1)}, u32[]{:S(2)}, u32[]{:S(2)}) collective-permute-start(bf16[128,1792]{1,0:T(8,128)(2,1)S(1)} %pad_maximum_fusion.1.refs_0_), channel_id=1, source_target_pairs={{0,2},{2,0},{4,6},{6,4},{8,10},{10,8},{12,14},{14,12},{16,18},{18,... | collective-permute-start | bytes 1376264 | tf_op jit(solution)/shard_map/ppermute | solution.py:30
  82.2 15.4 %collective-permute-start.30 = (bf16[128,1792]{1,0:T(8,128)(2,1)S(1)}, bf16[128,1792]{1,0:T(8,128)(2,1)S(1)}, u32[]{:S(2)}, u32[]{:S(2)}) collective-permute-start(bf16[128,1792]{1,0:T(8,128)(2,1)S(1)} %pad_maximum_fusion.1.refs_0_), channel_id=1, source_target_pairs={{0,4},{2,6},{4,0},{6,2},{8,12},{10,14},{12,8},{14,10},{16,20},{18,... | collective-permute-start | bytes 1376264 | tf_op jit(solution)/shard_map/ppermute | solution.py:30
  88.5 2.2 slice-start
  88.7 3.1 %slice-start.1 = ((s8[7340032]{0:T(1024)(128)(4,1)}), s8[3145728]{0:T(1024)(128)(4,1)S(1)}, s32[]{:S(2)}) async-start(s8[7340032]{0:T(1024)(128)(4,1)} %bitcast.72), calls=%async_computation.1 | async-start | bytes 6291456
  92.9 28.6 %collective-permute-start.23 = (bf16[128,1792]{1,0:T(8,128)(2,1)S(1)}, bf16[128,1792]{1,0:T(8,128)(2,1)S(1)}, u32[]{:S(2)}, u32[]{:S(2)}) collective-permute-start(bf16[128,1792]{1,0:T(8,128)(2,1)S(1)} %slice.435), channel_id=1, source_target_pairs={{0,8},{2,10},{4,12},{6,14},{8,16},{10,18},{12,20},{14,22},{16,24},... | collective-permute-start | bytes 1376264 | tf_op jit(solution)/shard_map/ppermute | solution.py:30
  94.3 53.9 %collective-permute-start.22 = (bf16[128,1792]{1,0:T(8,128)(2,1)S(1)}, bf16[128,1792]{1,0:T(8,128)(2,1)S(1)}, u32[]{:S(2)}, u32[]{:S(2)}) collective-permute-start(bf16[128,1792]{1,0:T(8,128)(2,1)S(1)} %get-tuple-element.91), channel_id=1, source_target_pairs={{0,16},{2,18},{4,20},{6,22},{8,24},{10,26},{12,28},{14,30},{16,0},... | collective-permute-start | bytes 1376264 | tf_op jit(solution)/shard_map/ppermute | solution.py:30
  94.3 56.3 %collective-permute-start.21 = (bf16[128,1792]{1,0:T(8,128)(2,1)S(1)}, bf16[128,1792]{1,0:T(8,128)(2,1)S(1)}, u32[]{:S(2)}, u32[]{:S(2)}) collective-permute-start(bf16[128,1792]{1,0:T(8,128)(2,1)S(1)} %get-tuple-element.90), channel_id=1, source_target_pairs={{0,24},{2,26},{4,28},{6,30},{8,0},{10,2},{12,4},{14,6},{16,8},{18,... | collective-permute-start | bytes 1376264 | tf_op jit(solution)/shard_map/ppermute | solution.py:30
  97.7 65.2 %collective-permute-start.35 = (bf16[128,1792]{1,0:T(8,128)(2,1)S(1)}, bf16[128,1792]{1,0:T(8,128)(2,1)S(1)}, u32[]{:S(2)}, u32[]{:S(2)}) collective-permute-start(bf16[128,1792]{1,0:T(8,128)(2,1)S(1)} %pad_maximum_fusion.2.refs_4_), channel_id=1, source_target_pairs={{0,8},{2,10},{4,12},{6,14},{8,16},{10,18},{12,20},{14,22},{16,24},... | collective-permute-start | bytes 1376264 | tf_op jit(solution)/shard_map/ppermute | solution.py:30
  121.6 47.0 %collective-permute-start.36 = (bf16[128,1792]{1,0:T(8,128)(2,1)S(1)}, bf16[128,1792]{1,0:T(8,128)(2,1)S(1)}, u32[]{:S(2)}, u32[]{:S(2)}) collective-permute-start(bf16[128,1792]{1,0:T(8,128)(2,1)S(1)} %pad_maximum_fusion.2.refs_4_), channel_id=1, source_target_pairs={{0,16},{2,18},{4,20},{6,22},{8,24},{10,26},{12,28},{14,30},{16,0},... | collective-permute-start | bytes 1376264 | tf_op jit(solution)/shard_map/ppermute | solution.py:30
  148.2 22.1 %collective-permute-start.37 = (bf16[128,1792]{1,0:T(8,128)(2,1)S(1)}, bf16[128,1792]{1,0:T(8,128)(2,1)S(1)}, u32[]{:S(2)}, u32[]{:S(2)}) collective-permute-start(bf16[128,1792]{1,0:T(8,128)(2,1)S(1)} %pad_maximum_fusion.2.refs_4_), channel_id=1, source_target_pairs={{0,24},{2,26},{4,28},{6,30},{8,0},{10,2},{12,4},{14,6},{16,8},{18,... | collective-permute-start | bytes 1376264 | tf_op jit(solution)/shard_map/ppermute | solution.py:30
  150.6 19.6 %collective-permute-start.31 = (bf16[128,1792]{1,0:T(8,128)(2,1)S(1)}, bf16[128,1792]{1,0:T(8,128)(2,1)S(1)}, u32[]{:S(2)}, u32[]{:S(2)}) collective-permute-start(bf16[128,1792]{1,0:T(8,128)(2,1)S(1)} %collective-permute-done.30.refs_2_), channel_id=1, source_target_pairs={{0,2},{2,0},{4,6},{6,4},{8,10},{10,8},{12,14},{14,12},{16,18},{18,... | collective-permute-start | bytes 1376264 | tf_op jit(solution)/shard_map/ppermute | solution.py:30
  152.1 31.5 %slice-start.2 = ((s8[7340032]{0:T(1024)(128)(4,1)}), s8[4194304]{0:T(1024)(128)(4,1)S(1)}, s32[]{:S(2)}) async-start(s8[7340032]{0:T(1024)(128)(4,1)} %bitcast.74), calls=%async_computation.2 | async-start | bytes 8388608
  152.3 31.3 %collective-permute-start.16 = (bf16[256,1792]{1,0:T(8,128)(2,1)S(1)}, bf16[256,1792]{1,0:T(8,128)(2,1)S(1)}, u32[]{:S(2)}, u32[]{:S(2)}) collective-permute-start(bf16[256,1792]{1,0:T(8,128)(2,1)S(1)} %fusion.54), channel_id=1, source_target_pairs={{0,4},{2,6},{4,0},{6,2},{8,12},{10,14},{12,8},{14,10},{16,20},{18,... | collective-permute-start | bytes 2752520 | tf_op jit(solution)/shard_map/ppermute | solution.py:30
  162.9 15.0 %collective-permute-start.24 = (bf16[64,1792]{1,0:T(8,128)(2,1)S(1)}, bf16[64,1792]{1,0:T(8,128)(2,1)S(1)}, u32[]{:S(2)}, u32[]{:S(2)}) collective-permute-start(bf16[64,1792]{1,0:T(8,128)(2,1)S(1)} %concatenate.81), channel_id=1, source_target_pairs={{0,2},{2,0},{4,6},{6,4},{8,10},{10,8},{12,14},{14,12},{16,18},{18,... | collective-permute-start | bytes 688136 | tf_op jit(solution)/shard_map/ppermute | solution.py:30
  170.2 13.4 %slice-start.3 = ((s8[7340032]{0:T(1024)(128)(4,1)}), s8[3145728]{0:T(1024)(128)(4,1)S(1)}, s32[]{:S(2)}) async-start(s8[7340032]{0:T(1024)(128)(4,1)} %bitcast.74), calls=%async_computation.3 | async-start | bytes 6291456
  177.8 8.6 %collective-permute-start.38 = (bf16[512,1024]{1,0:T(8,128)(2,1)S(1)}, bf16[512,1024]{1,0:T(8,128)(2,1)S(1)}, u32[]{:S(2)}, u32[]{:S(2)}) collective-permute-start(bf16[512,1024]{1,0:T(8,128)(2,1)S(1)} %shard_map.87), channel_id=1, source_target_pairs={{0,1},{1,0},{2,3},{3,2},{4,5},{5,4},{6,7},{7,6},{8,9},{9,8},{10,11... | collective-permute-start | bytes 3145736 | tf_op jit(solution)/shard_map/ppermute | solution.py:30
  177.9 5.6 %collective-permute-start.25 = (bf16[32,1792]{1,0:T(8,128)(2,1)S(1)}, bf16[32,1792]{1,0:T(8,128)(2,1)S(1)}, u32[]{:S(2)}, u32[]{:S(2)}) collective-permute-start(bf16[32,1792]{1,0:T(8,128)(2,1)S(1)} %add_convert_fusion.2), channel_id=1, source_target_pairs={{0,4},{2,6},{4,0},{6,2},{8,12},{10,14},{12,8},{14,10},{16,20},{18,... | collective-permute-start | bytes 344072 | tf_op jit(solution)/shard_map/ppermute | solution.py:30
  183.6 4.3 %slice-start.4 = ((s8[7340032]{0:T(1024)(128)(4,1)}), s8[3145728]{0:T(1024)(128)(4,1)S(1)}, s32[]{:S(2)}) async-start(s8[7340032]{0:T(1024)(128)(4,1)} %bitcast.77), calls=%async_computation.4 | async-start | bytes 6291456
  184.9 3.0 %slice-start.5 = ((s8[7340032]{0:T(1024)(128)(4,1)}), s8[4194304]{0:T(1024)(128)(4,1)S(1)}, s32[]{:S(2)}) async-start(s8[7340032]{0:T(1024)(128)(4,1)} %bitcast.77), calls=%async_computation.5 | async-start | bytes 8388608
  184.9 16.9 %collective-permute-start.17 = (bf16[128,1792]{1,0:T(8,128)(2,1)S(1)}, bf16[128,1792]{1,0:T(8,128)(2,1)S(1)}, u32[]{:S(2)}, u32[]{:S(2)}) collective-permute-start(bf16[128,1792]{1,0:T(8,128)(2,1)S(1)} %slice.666), channel_id=1, source_target_pairs={{0,2},{2,0},{4,6},{6,4},{8,10},{10,8},{12,14},{14,12},{16,18},{18,... | collective-permute-start | bytes 1376264 | tf_op jit(solution)/shard_map/ppermute | solution.py:30
  187.8 2.2 slice-start.6
  187.9 3.0 %slice-start.7 = ((s8[7340032]{0:T(1024)(128)(4,1)}), s8[3145728]{0:T(1024)(128)(4,1)S(1)}, s32[]{:S(2)}) async-start(s8[7340032]{0:T(1024)(128)(4,1)} %bitcast.80), calls=%async_computation.7 | async-start | bytes 6291456
  192.3 20.5 %collective-permute-start.39 = (bf16[128,1792]{1,0:T(8,128)(2,1)S(1)}, bf16[128,1792]{1,0:T(8,128)(2,1)S(1)}, u32[]{:S(2)}, u32[]{:S(2)}) collective-permute-start(bf16[128,1792]{1,0:T(8,128)(2,1)S(1)} %get-tuple-element.83), channel_id=1, source_target_pairs={{0,4},{2,6},{4,0},{6,2},{8,12},{10,14},{12,8},{14,10},{16,20},{18,... | collective-permute-start | bytes 1376264 | tf_op jit(solution)/shard_map/ppermute | solution.py:30
  198.5 15.5 %collective-permute-start.41 = (bf16[128,1792]{1,0:T(8,128)(2,1)S(1)}, bf16[128,1792]{1,0:T(8,128)(2,1)S(1)}, u32[]{:S(2)}, u32[]{:S(2)}) collective-permute-start(bf16[128,1792]{1,0:T(8,128)(2,1)S(1)} %get-tuple-element.85), channel_id=1, source_target_pairs={{0,2},{2,0},{4,6},{6,4},{8,10},{10,8},{12,14},{14,12},{16,18},{18,... | collective-permute-start | bytes 1376264 | tf_op jit(solution)/shard_map/ppermute | solution.py:30
  202.0 6.1 %collective-permute-start.20 = (bf16[32,1792]{1,0:T(8,128)(2,1)S(1)}, bf16[32,1792]{1,0:T(8,128)(2,1)S(1)}, u32[]{:S(2)}, u32[]{:S(2)}) collective-permute-start(bf16[32,1792]{1,0:T(8,128)(2,1)S(1)} %get-tuple-element.95), channel_id=1, source_target_pairs={{0,8},{2,10},{4,12},{6,14},{8,16},{10,18},{12,20},{14,22},{16,24},... | collective-permute-start | bytes 344072 | tf_op jit(solution)/shard_map/ppermute | solution.py:30
  202.1 8.9 %collective-permute-start.19 = (bf16[32,1792]{1,0:T(8,128)(2,1)S(1)}, bf16[32,1792]{1,0:T(8,128)(2,1)S(1)}, u32[]{:S(2)}, u32[]{:S(2)}) collective-permute-start(bf16[32,1792]{1,0:T(8,128)(2,1)S(1)} %get-tuple-element.96), channel_id=1, source_target_pairs={{0,16},{2,18},{4,20},{6,22},{8,24},{10,26},{12,28},{14,30},{16,0},... | collective-permute-start | bytes 344072 | tf_op jit(solution)/shard_map/ppermute | solution.py:30
  202.7 10.1 %collective-permute-start.18 = (bf16[32,1792]{1,0:T(8,128)(2,1)S(1)}, bf16[32,1792]{1,0:T(8,128)(2,1)S(1)}, u32[]{:S(2)}, u32[]{:S(2)}) collective-permute-start(bf16[32,1792]{1,0:T(8,128)(2,1)S(1)} %get-tuple-element.94), channel_id=1, source_target_pairs={{0,24},{2,26},{4,28},{6,30},{8,0},{10,2},{12,4},{14,6},{16,8},{18,... | collective-permute-start | bytes 344072 | tf_op jit(solution)/shard_map/ppermute | solution.py:30
  208.1 13.7 %collective-permute-start.45 = (bf16[128,1792]{1,0:T(8,128)(2,1)S(1)}, bf16[128,1792]{1,0:T(8,128)(2,1)S(1)}, u32[]{:S(2)}, u32[]{:S(2)}) collective-permute-start(bf16[128,1792]{1,0:T(8,128)(2,1)S(1)} %get-tuple-element.84), channel_id=1, source_target_pairs={{0,2},{2,0},{4,6},{6,4},{8,10},{10,8},{12,14},{14,12},{16,18},{18,... | collective-permute-start | bytes 1376264 | tf_op jit(solution)/shard_map/ppermute | solution.py:30
  211.0 11.8 %collective-permute-start.43 = (bf16[128,1792]{1,0:T(8,128)(2,1)S(1)}, bf16[128,1792]{1,0:T(8,128)(2,1)S(1)}, u32[]{:S(2)}, u32[]{:S(2)}) collective-permute-start(bf16[128,1792]{1,0:T(8,128)(2,1)S(1)} %get-tuple-element.82), channel_id=1, source_target_pairs={{0,4},{2,6},{4,0},{6,2},{8,12},{10,14},{12,8},{14,10},{16,20},{18,... | collective-permute-start | bytes 1376264 | tf_op jit(solution)/shard_map/ppermute | solution.py:30
  212.9 13.7 %collective-permute-start.40 = (bf16[64,1792]{1,0:T(8,128)(2,1)S(1)}, bf16[64,1792]{1,0:T(8,128)(2,1)S(1)}, u32[]{:S(2)}, u32[]{:S(2)}) collective-permute-start(bf16[64,1792]{1,0:T(8,128)(2,1)S(1)} %slice.670), channel_id=1, source_target_pairs={{0,2},{2,0},{4,6},{6,4},{8,10},{10,8},{12,14},{14,12},{16,18},{18,... | collective-permute-start | bytes 688136 | tf_op jit(solution)/shard_map/ppermute | solution.py:30
  214.1 12.7 %collective-permute-start.42 = (bf16[64,1792]{1,0:T(8,128)(2,1)S(1)}, bf16[64,1792]{1,0:T(8,128)(2,1)S(1)}, u32[]{:S(2)}, u32[]{:S(2)}) collective-permute-start(bf16[64,1792]{1,0:T(8,128)(2,1)S(1)} %slice.669), channel_id=1, source_target_pairs={{0,4},{2,6},{4,0},{6,2},{8,12},{10,14},{12,8},{14,10},{16,20},{18,... | collective-permute-start | bytes 688136 | tf_op jit(solution)/shard_map/ppermute | solution.py:30
  221.9 7.7 %collective-permute-start.46 = (bf16[64,1792]{1,0:T(8,128)(2,1)S(1)}, bf16[64,1792]{1,0:T(8,128)(2,1)S(1)}, u32[]{:S(2)}, u32[]{:S(2)}) collective-permute-start(bf16[64,1792]{1,0:T(8,128)(2,1)S(1)} %slice.667), channel_id=1, source_target_pairs={{0,4},{2,6},{4,0},{6,2},{8,12},{10,14},{12,8},{14,10},{16,20},{18,... | collective-permute-start | bytes 688136 | tf_op jit(solution)/shard_map/ppermute | solution.py:30
  222.9 6.7 %collective-permute-start.44 = (bf16[64,1792]{1,0:T(8,128)(2,1)S(1)}, bf16[64,1792]{1,0:T(8,128)(2,1)S(1)}, u32[]{:S(2)}, u32[]{:S(2)}) collective-permute-start(bf16[64,1792]{1,0:T(8,128)(2,1)S(1)} %slice.668), channel_id=1, source_target_pairs={{0,2},{2,0},{4,6},{6,4},{8,10},{10,8},{12,14},{14,12},{16,18},{18,... | collective-permute-start | bytes 688136 | tf_op jit(solution)/shard_map/ppermute | solution.py:30
  226.9 18.1 %collective-permute-start.49 = (bf16[32,3584]{1,0:T(8,128)(2,1)S(1)}, bf16[32,3584]{1,0:T(8,128)(2,1)S(1)}, u32[]{:S(2)}, u32[]{:S(2)}) collective-permute-start(bf16[32,3584]{1,0:T(8,128)(2,1)S(1)} %fusion.90), channel_id=1, source_target_pairs={{0,8},{2,10},{4,12},{6,14},{8,16},{10,18},{12,20},{14,22},{16,24},... | collective-permute-start | bytes 688136 | tf_op jit(solution)/shard_map/ppermute | solution.py:30
  229.8 17.7 %collective-permute-start.48 = (bf16[32,3584]{1,0:T(8,128)(2,1)S(1)}, bf16[32,3584]{1,0:T(8,128)(2,1)S(1)}, u32[]{:S(2)}, u32[]{:S(2)}) collective-permute-start(bf16[32,3584]{1,0:T(8,128)(2,1)S(1)} %get-tuple-element.93), channel_id=1, source_target_pairs={{0,16},{2,18},{4,20},{6,22},{8,24},{10,26},{12,28},{14,30},{16,0},... | collective-permute-start | bytes 688136 | tf_op jit(solution)/shard_map/ppermute | solution.py:30
  233.0 17.5 %collective-permute-start.47 = (bf16[32,3584]{1,0:T(8,128)(2,1)S(1)}, bf16[32,3584]{1,0:T(8,128)(2,1)S(1)}, u32[]{:S(2)}, u32[]{:S(2)}) collective-permute-start(bf16[32,3584]{1,0:T(8,128)(2,1)S(1)} %get-tuple-element.92), channel_id=1, source_target_pairs={{0,24},{2,26},{4,28},{6,30},{8,0},{10,2},{12,4},{14,6},{16,8},{18,... | collective-permute-start | bytes 688136 | tf_op jit(solution)/shard_map/ppermute | solution.py:30
